TPU v7x, 32 devices: a whole 2x2x4 slice. The times are simulated.
32 devices in a mesh: grp: 2 (over x), wave: 16 (over z, y, core).
Axes of the slice: x: 2, y: 2, z: 4, core: 2. Of those that a mesh axis runs over, the one named last changes fastest.
Arguments:
- north_rows: bfloat16 [2560, 128, 274], P(('grp', 'wave')), parts along dimension 0, may hold values from -6 to 6
- south_rows: bfloat16 [2560, 128, 274], P(('grp', 'wave')), parts along dimension 0, may hold values from -6 to 6
- lon_counts: int32 [1280], replicated, may hold values from 20 to 5148, as said below
- slot_wave: int32 [128], replicated, may hold values from 0 to 2559, as said below
- legendre: bfloat16 [128, 1280, 1280], P('wave'), may hold values from -0.15625 to 0.15625
- mode_rates: float32 [137], replicated, may hold values from 0.05 to 20
- to_modes: bfloat16 [137, 137], replicated, may hold values from -0.5 to 0.5
- from_modes: bfloat16 [137, 137], replicated, may hold values from -0.5 to 0.5
Outputs:
- spec_state: bfloat16 [256, 1280, 274], P(('grp', 'wave')), parts along dimension 0
- new_rows: bfloat16 [2560, 128, 274], P(('grp', 'wave')), parts along dimension 0
There are 2 independent parts, one for each index of `grp`. A program takes and returns all parts, laid end to end along the dimension named above; an argument that names none is the same for every part. Nothing has to cross between parts.
Inputs may be any that keep to these rules, and one draw needn't show every extreme that they name: Wavenumber m is present in latitude row j only if 2 m is below lon_counts[j]. `slot_wave`: distinct zonal wavenumbers.
All inputs are finite; a program needn't handle non-finite values.
Results may differ from a plain program's by a relative error of at most 0.0065.
Values may be sent and summed in bfloat16 or wider, within the bound.
A program may use at most 192 MiB of HBM per device.

v0:
```python
import jax
import jax.numpy as jnp
from jax import lax
from jax.sharding import PartitionSpec as P

NMAX = 2559


def vertical_step(direct, own_waves, mode_rates, to_modes, from_modes):
    slot_count, row_total, channels = direct.shape
    levels = to_modes.shape[0]
    modal_part = jnp.dot(direct.reshape(-1, levels), to_modes, preferred_element_type=jnp.float32)
    modal_part = modal_part.reshape(slot_count, row_total, 2, levels)
    degree = own_waves[:, None] + 2 * jnp.arange(row_total, dtype=jnp.int32)[None, :]
    degree_f = degree.astype(jnp.float32)
    scaled_degree = degree_f * (degree_f + 1.0) / float(NMAX * (NMAX + 1))
    divisor = 1.0 + mode_rates[None, None, None, :] * scaled_degree[:, :, None, None]
    scaled = (modal_part / divisor).astype(jnp.bfloat16).reshape(-1, levels)
    result = jnp.dot(scaled, from_modes, preferred_element_type=jnp.float32)
    result = result.reshape(slot_count, row_total, channels)
    return jnp.where((degree <= NMAX)[:, :, None], result, 0.0).astype(jnp.bfloat16)


def per_device(
    north_rows, south_rows, lon_counts, slot_wave, legendre, mode_rates, to_modes, from_modes
):
    lat_dev = north_rows.shape[0]
    slot_dev, row_total, lat_total = legendre.shape
    my_index = lax.axis_index("wave")
    own_waves = lax.dynamic_slice_in_dim(slot_wave, my_index * slot_dev, slot_dev)
    live_own = 2 * own_waves[None, :] < lon_counts[:, None]
    local_counts = lax.dynamic_slice_in_dim(lon_counts, my_index * lat_dev, lat_dev)
    live_here = 2 * slot_wave[None, :] < local_counts[:, None]
    summed = north_rows.astype(jnp.float32) + south_rows.astype(jnp.float32)
    sym_here = jnp.where(live_here[:, :, None], summed, 0.0).astype(jnp.bfloat16)
    columns = lax.all_to_all(sym_here, "wave", split_axis=1, concat_axis=0, tiled=True)
    direct = jnp.einsum(
        "snj,jsc->snc", legendre, columns, preferred_element_type=jnp.float32
    ).astype(jnp.bfloat16)
    spec_state = vertical_step(direct, own_waves, mode_rates, to_modes, from_modes)
    returned = jnp.einsum("snj,snc->jsc", legendre, spec_state, preferred_element_type=jnp.float32)
    returned = jnp.where(live_own[:, :, None], returned, 0.0).astype(jnp.bfloat16)
    new_rows = lax.all_to_all(returned, "wave", split_axis=0, concat_axis=1, tiled=True)
    return (spec_state, new_rows)


def solution(mesh):
    in_specs = (
        P(("grp", "wave"), None, None),
        P(("grp", "wave"), None, None),
        P(),
        P(),
        P("wave", None, None),
        P(),
        P(),
        P(),
    )
    out_specs = (P(("grp", "wave"), None, None), P(("grp", "wave"), None, None))
    return jax.shard_map(
        per_device, mesh=mesh, in_specs=in_specs, out_specs=out_specs, check_vma=False
    )
```

profile of v0, /device:TPU:13, one launch (start us, length us, event | category | flops | bytes accessed | tf_op | source)
XLA Modules:
  0.0 580.0 jit_solution(6979879642193113835)
XLA Ops:
  0.6 0.0 copy-start
  0.7 11.0 %copy.45 = bf16[80,128,274]{2,0,1:T(8,128)(2,1)} copy(bf16[80,128,274]{1,0,2:T(8,128)(2,1)} %param.9) | data formatting | bytes 11223040 | tf_op args[1]
  11.6 0.0 copy-start.5
  11.6 0.0 copy-start.3
  11.6 11.0 %copy.44 = bf16[80,128,274]{2,0,1:T(8,128)(2,1)} copy(bf16[80,128,274]{1,0,2:T(8,128)(2,1)} %param.8) | data formatting | bytes 11223040 | tf_op args[0]
  22.7 0.0 copy-done.5
  22.7 0.0 copy-done.3
  22.7 0.1 dynamic_slice.7
  22.8 0.1 broadcast_compare_fusion
  22.9 9.6 %select_convert_fusion.1 = bf16[80,128,274]{2,0,1:T(8,128)(2,1)} fusion(bf16[80,128,274]{2,0,1:T(8,128)(2,1)} %copy.45, bf16[80,128,274]{2,0,1:T(8,128)(2,1)} %copy.44, pred[80,128]{0,1:T(8,128)(4,1)S(1)} %broadcast_compare_fusion), kind=kLoop, calls=%fused_computation.1 | loop fusion | flops 14028800 | bytes 16844800 | tf_op jit(solution)/shard_map/convert_element_type | solution.py:35
  32.5 0.0 copy-start.4
  32.5 6.7 %all-to-all-start = ((bf16[80,128,274]{2,0,1:T(8,128)(2,1)}), bf16[80,128,274]{2,0,1:T(8,128)(2,1)}, u32[]{:S(2)}, u32[]{:S(2)}) async-start(bf16[80,128,274]{2,0,1:T(8,128)(2,1)} %select_convert_fusion.1), calls=%async_computation | async-start | bytes 15728640 | tf_op jit(solution)/shard_map/all_to_all | solution.py:36
  39.2 0.1 broadcast_multiply_fusion
  39.2 0.1 broadcast_compare_fusion.1
  39.3 0.1 add_compare_fusion
  39.4 0.1 fusion.3
  39.5 0.0 copy-done.4
  39.5 3.2 multiply_add_fusion
  42.7 167.6 %all-to-all-done = bf16[80,128,274]{2,0,1:T(8,128)(2,1)} async-done(((bf16[80,128,274]{2,0,1:T(8,128)(2,1)}), bf16[80,128,274]{2,0,1:T(8,128)(2,1)}, u32[]{:S(2)}, u32[]{:S(2)}) %all-to-all-start) | async-done | bytes 5611552 | tf_op jit(solution)/shard_map/all_to_all | solution.py:36
  210.3 14.5 %copy.65 = bf16[16,80,8,274]{1,0,3,2:T(8,128)(2,1)} copy(bf16[16,80,8,274]{3,1,2,0:T(8,128)(2,1)} %bitcast.2) | data formatting | bytes 11223040 | tf_op jit(solution)/shard_map/all_to_all | solution.py:36
  224.8 13.2 %reshape.146 = bf16[1280,8,274]{0,2,1:T(8,128)(2,1)} reshape(bf16[16,80,8,274]{1,0,3,2:T(8,128)(2,1)} %copy.65) | data formatting | bytes 11223040 | tf_op jit(solution)/shard_map/all_to_all | solution.py:36
  238.0 25.7 %convert_bitcast_fusion = bf16[8,1280,274]{1,2,0:T(8,128)(2,1)} fusion(bf16[1280,8,274]{0,2,1:T(8,128)(2,1)} %reshape.146, bf16[8,1280,1280]{2,1,0:T(8,128)(2,1)} %param.12), kind=kOutput, calls=%fused_computation.8 | convolution fusion | flops 7185551360 | bytes 37437440 | tf_op jit(solution)/shard_map/snj,jsc->snc/dot_general | solution.py:37
  263.7 3.7 copy.49
  267.4 0.0 copy-done
  267.4 6.4 %divide_convert_fusion = bf16[8,1280,2,137]{1,3,2,0:T(8,128)(2,1)} fusion(bf16[8,1280,2,137]{1,0,3,2:T(8,128)(2,1)S(1)} %bitcast.31, f32[8,1280,137]{1,2,0:T(8,128)} %multiply_add_fusion, bf16[137,137]{1,0:T(8,128)(2,1)S(1)} %copy-done), kind=kOutput, calls=%fused_computation.2 | convolution fusion | flops 774389760 | bytes 16872098 | tf_op jit(solution)/shard_map/dot_general | solution.py:12
  273.8 25.2 %copy.52 = bf16[8,1280,2,137]{3,2,1,0:T(2,128)(2,1)} copy(bf16[8,1280,2,137]{1,3,2,0:T(8,128)(2,1)} %divide_convert_fusion) | data formatting | bytes 11223040 | tf_op jit(solution)/shard_map/convert_element_type | solution.py:18
  299.1 0.0 copy-start.2
  299.1 18.9 %reshape.143 = bf16[20480,137]{1,0:T(8,128)(2,1)} reshape(bf16[8,1280,2,137]{3,2,1,0:T(2,128)(2,1)} %copy.52) | data formatting | bytes 11223040 | tf_op jit(solution)/shard_map/reshape | solution.py:18
  318.0 0.0 copy-done.2
  318.0 10.8 %fusion.4 = bf16[20480,137]{1,0:T(8,128)(2,1)} fusion(bf16[20480,137]{1,0:T(8,128)(2,1)} %reshape.143, bf16[137,137]{1,0:T(8,128)(2,1)S(1)} %copy-done.2), kind=kOutput, calls=%fused_computation.19 | convolution fusion | flops 768778240 | bytes 11260578 | tf_op jit(solution)/shard_map/dot_general | solution.py:19
  328.8 16.0 %reshape.144 = bf16[8,1280,274]{2,1,0:T(8,128)(2,1)} reshape(bf16[20480,137]{1,0:T(8,128)(2,1)} %fusion.4) | data formatting | bytes 11223040 | tf_op jit(solution)/shard_map/reshape | solution.py:20
  344.8 7.6 %select_convert_fusion = bf16[8,1280,274]{2,1,0:T(8,128)(2,1)} fusion(bf16[8,1280,274]{2,1,0:T(8,128)(2,1)} %reshape.144, pred[8,1280]{1,0:T(8,128)(4,1)S(1)} %add_compare_fusion), kind=kLoop, calls=%fused_computation | loop fusion | flops 2805760 | bytes 11233280 | tf_op jit(solution)/shard_map/convert_element_type | solution.py:21
  352.4 16.3 %fusion.5 = bf16[8,274,1280]{2,1,0:T(8,128)(2,1)} fusion(bf16[8,1280,274]{2,1,0:T(8,128)(2,1)} %select_convert_fusion, bf16[8,1280,1280]{2,1,0:T(8,128)(2,1)} %param.12), kind=kOutput, calls=%fused_computation.20 | convolution fusion | flops 7182745600 | bytes 37437440 | tf_op jit(solution)/shard_map/snj,snc->jsc/dot_general | solution.py:41
  368.7 6.5 %fusion = bf16[1280,8,274]{0,1,2:T(8,128)(2,1)} fusion(bf16[8,274,1280]{2,1,0:T(8,128)(2,1)} %fusion.5, pred[1280,8]{0,1:T(8,128)(4,1)S(1)} %broadcast_compare_fusion.1), kind=kLoop, calls=%fused_computation.4 | loop fusion | flops 2805760 | bytes 11233280 | tf_op jit(solution)/shard_map/convert_element_type | solution.py:42
  375.2 10.9 %copy.56 = bf16[1280,8,274]{2,1,0:T(8,128)(2,1)} copy(bf16[1280,8,274]{0,1,2:T(8,128)(2,1)} %fusion) | data formatting | bytes 11223040 | tf_op jit(solution)/shard_map/convert_element_type | solution.py:42
  386.2 4.8 all-to-all-start.1
  391.0 10.1 %copy.59 = bf16[8,1280,274]{1,0,2:T(8,128)(2,1)} copy(bf16[8,1280,274]{2,1,0:T(8,128)(2,1)} %select_convert_fusion) | data formatting | bytes 11223040
  401.0 161.1 %all-to-all-done.1 = bf16[1280,8,274]{2,1,0:T(8,128)(2,1)} async-done(((bf16[1280,8,274]{2,1,0:T(8,128)(2,1)}), bf16[1280,8,274]{2,1,0:T(8,128)(2,1)}, u32[]{:S(2)}, u32[]{:S(2)}) %all-to-all-start.1) | async-done | bytes 5611552 | tf_op jit(solution)/shard_map/all_to_all | solution.py:43
  562.1 0.0 copy-start.1
  562.1 7.9 %copy.74 = bf16[80,16,8,274]{3,2,1,0:T(8,128)(2,1)} copy(bf16[80,16,8,274]{3,2,0,1:T(8,128)(2,1)} %bitcast.9) | data formatting | bytes 11223040 | tf_op jit(solution)/shard_map/all_to_all | solution.py:43
  570.0 10.0 %copy.60 = bf16[80,128,274]{1,0,2:T(8,128)(2,1)} copy(bf16[80,128,274]{2,1,0:T(8,128)(2,1)} %bitcast.30) | data formatting | bytes 11223040
  580.0 0.0 copy-done.1
  (2 shorter events, 0.0 us)
Async XLA Ops:
  0.6 266.8 %copy-start = (bf16[137,137]{1,0:T(8,128)(2,1)S(1)}, bf16[137,137]{1,0:T(8,128)(2,1)}, u32[]{:S(2)}) copy-start(bf16[137,137]{1,0:T(8,128)(2,1)} %param.14) | copy-start | bytes 112618
  11.6 11.1 %copy-start.5 = (s32[128]{0:T(128)S(1)}, s32[128]{0:T(128)}, u32[]{:S(2)}) copy-start(s32[128]{0:T(128)} %param.11) | copy-start | bytes 1540
  11.6 11.1 %copy-start.3 = (s32[1280]{0:T(1024)S(1)}, s32[1280]{0:T(1024)}, u32[]{:S(2)}) copy-start(s32[1280]{0:T(1024)} %param.10) | copy-start | bytes 15364
  32.5 7.0 %copy-start.4 = (f32[137]{0:T(256)S(1)}, f32[137]{0:T(256)}, u32[]{:S(2)}) copy-start(f32[137]{0:T(256)} %param.13) | copy-start | bytes 1648
  32.5 177.8 %all-to-all-start = ((bf16[80,128,274]{2,0,1:T(8,128)(2,1)}), bf16[80,128,274]{2,0,1:T(8,128)(2,1)}, u32[]{:S(2)}, u32[]{:S(2)}) async-start(bf16[80,128,274]{2,0,1:T(8,128)(2,1)} %select_convert_fusion.1), calls=%async_computation | async-start | bytes 15728640 | tf_op jit(solution)/shard_map/all_to_all | solution.py:36
  299.1 18.9 %copy-start.2 = (bf16[137,137]{1,0:T(8,128)(2,1)S(1)}, bf16[137,137]{1,0:T(8,128)(2,1)}, u32[]{:S(2)}) copy-start(bf16[137,137]{1,0:T(8,128)(2,1)} %param.15) | copy-start | bytes 112618
  386.2 175.9 %all-to-all-start.1 = ((bf16[1280,8,274]{2,1,0:T(8,128)(2,1)}), bf16[1280,8,274]{2,1,0:T(8,128)(2,1)}, u32[]{:S(2)}, u32[]{:S(2)}) async-start(bf16[1280,8,274]{2,1,0:T(8,128)(2,1)} %copy.56), calls=%async_computation.1 | async-start | bytes 15728640 | tf_op jit(solution)/shard_map/all_to_all | solution.py:43
  562.1 17.9 %copy-start.1 = (bf16[137,137]{1,0:T(8,128)(2,1)S(1)}, bf16[137,137]{1,0:T(8,128)(2,1)}, u32[]{:S(2)}) copy-start(bf16[137,137]{1,0:T(8,128)(2,1)} %param.14) | copy-start | bytes 112618
where the time goes:
time: 584 us; the launch traced here: 580 us
  waiting for transfers between devices  329 us (56%)
  local copies, waits for them, and re-layouts  153 us (26%)
  matrix products  59.3 us (10%)
  other arithmetic  27.3 us (5%)
  starting transfers between devices  11.4 us (2%)
    all_to_all x1, waiting for transfers between devices, per_device(): lax.all_to_all(sym_here, 'wave', split_axis=1, concat_axis=0, tiled=True)  168 us
    all_to_all x1, waiting for transfers between devices, per_device(): lax.all_to_all(returned, 'wave', split_axis=0, concat_axis=1, tiled=True)  161 us
    unnamed x16, local copies, waits for them, and re-layouts  42.2 us
    all_to_all x2, local copies, waits for them, and re-layouts, per_device(): lax.all_to_all(sym_here, 'wave', split_axis=1, concat_axis=0, tiled=True)  27.8 us
    dot_general x1, matrix products, per_device(): jnp.einsum('snj,jsc->snc', legendre, columns, preferred_element_type=jnp....  25.7 us
    convert_element_type x1, local copies, waits for them, and re-layouts, vertical_step(): scaled = (modal_part / divisor).astype(jnp.bfloat16).reshape(-1, levels)  25.2 us
    reshape x1, local copies, waits for them, and re-layouts, vertical_step(): scaled = (modal_part / divisor).astype(jnp.bfloat16).reshape(-1, levels)  18.9 us
    dot_general x1, matrix products, per_device(): jnp.einsum('snj,snc->jsc', legendre, spec_state, preferred_element_type=j...  16.3 us
  transfers between devices with their start and end apart: 2, of which 2 were waited for; matrix products, arithmetic and copies ran while one was open for 2% of the time, Pallas kernels for 0%

commit v1 on v0

v1 whole, which is shorter than its diff:
```python
import functools

import jax
import jax.numpy as jnp
from jax import lax
from jax.experimental import pallas as pl
from jax.experimental.pallas import tpu as pltpu
from jax.sharding import PartitionSpec as P

NMAX = 2559
VMEM_LIMIT = 60 * 1024 * 1024


def sum_kernel(counts_ref, waves_ref, north_ref, south_ref, out_ref):
    live = 2 * waves_ref[...] < counts_ref[...]
    total = north_ref[...].astype(jnp.float32) + south_ref[...].astype(jnp.float32)
    out_ref[...] = jnp.where(live[None], total, 0.0).astype(jnp.bfloat16)


def symmetric_part(part, levels, north, south, counts, waves):
    _, lats, slots = north.shape
    step = next((t for t in (16, 8) if lats % t == 0), lats)
    return pl.pallas_call(
        sum_kernel,
        grid=(lats // step,),
        in_specs=[
            pl.BlockSpec((step, 1), lambda g: (g, 0)),
            pl.BlockSpec((1, slots), lambda g: (0, 0)),
            pl.BlockSpec((levels, step, slots), lambda g: (part, g, 0)),
            pl.BlockSpec((levels, step, slots), lambda g: (part, g, 0)),
        ],
        out_specs=pl.BlockSpec((levels, step, slots), lambda g: (0, g, 0)),
        out_shape=jax.ShapeDtypeStruct((levels, lats, slots), jnp.bfloat16),
        name=f"sum{part}",
    )(counts, waves, north, south)


def pack_kernel(own, lats, in_ref, out_ref):
    for i in range(own):
        out_ref[0, :, lats * i : lats * (i + 1)] = in_ref[i]


def pack(rows, own):
    slots, levels, lats = rows.shape
    return pl.pallas_call(
        functools.partial(pack_kernel, own, lats),
        grid=(slots // own,),
        in_specs=[pl.BlockSpec((own, levels, lats), lambda d: (d, 0, 0))],
        out_specs=pl.BlockSpec((1, levels, own * lats), lambda d: (d, 0, 0)),
        out_shape=jax.ShapeDtypeStruct((slots // own, levels, own * lats), jnp.bfloat16),
        name="pack",
    )(rows)


def unpack_kernel(own, lats, in_ref, out_ref):
    for i in range(own):
        out_ref[i] = in_ref[0, :, lats * i : lats * (i + 1)]


def unpack(packed, own):
    senders, levels, width = packed.shape
    lats = width // own
    return pl.pallas_call(
        functools.partial(unpack_kernel, own, lats),
        grid=(senders,),
        in_specs=[pl.BlockSpec((1, levels, width), lambda d: (d, 0, 0))],
        out_specs=pl.BlockSpec((own, levels, lats), lambda d: (d, 0, 0)),
        out_shape=jax.ShapeDtypeStruct((senders * own, levels, lats), jnp.bfloat16),
        name="unpack",
    )(packed)


def compute_kernel(
    own, senders, lats, waves_ref, counts_ref, rates_ref, to_ref, from_ref, rows_ref, leg_ref,
    state_ref, back_ref, columns, returned,
):
    slot = pl.program_id(0)

    @pl.when(slot == 0)
    def _():
        for s in range(own):
            for d in range(senders):
                columns[s, :, lats * d : lats * (d + 1)] = rows_ref[d, :, lats * s : lats * (s + 1)]

    wave = waves_ref[slot]
    direct = lax.dot_general(
        columns[slot], leg_ref[0], (((1,), (1,)), ((), ())), preferred_element_type=jnp.float32
    ).astype(jnp.bfloat16)
    modal = jnp.dot(to_ref[...], direct, preferred_element_type=jnp.float32)
    degree = wave + 2 * lax.broadcasted_iota(jnp.int32, (1, leg_ref.shape[1]), 1)
    degree_f = degree.astype(jnp.float32)
    scaled_degree = degree_f * (degree_f + 1.0) / float(NMAX * (NMAX + 1))
    divisor = 1.0 + rates_ref[...] * scaled_degree
    scaled = (modal / divisor).astype(jnp.bfloat16)
    state = jnp.dot(from_ref[...], scaled, preferred_element_type=jnp.float32)
    state = jnp.where(degree <= NMAX, state, 0.0).astype(jnp.bfloat16)
    state_ref[0] = state
    back = jnp.dot(state, leg_ref[0], preferred_element_type=jnp.float32)
    returned[slot] = jnp.where(2 * wave < counts_ref[...], back, 0.0).astype(jnp.bfloat16)

    @pl.when(slot == own - 1)
    def _():
        for s in range(own):
            for d in range(senders):
                back_ref[d, :, lats * s : lats * (s + 1)] = returned[s, :, lats * d : lats * (d + 1)]


def compute(rows, legendre, own_waves, counts, rates, to_t, from_t):
    senders, levels, width = rows.shape
    own, row_total, lat_total = legendre.shape
    lats = lat_total // senders
    whole = lambda *shape: pl.BlockSpec(shape, lambda s, w: (0,) * len(shape))
    return pl.pallas_call(
        functools.partial(compute_kernel, own, senders, lats),
        grid_spec=pltpu.PrefetchScalarGridSpec(
            num_scalar_prefetch=1,
            grid=(own,),
            in_specs=[
                whole(1, lat_total),
                whole(levels, 1),
                whole(levels, levels),
                whole(levels, levels),
                whole(senders, levels, width),
                pl.BlockSpec((1, row_total, lat_total), lambda s, w: (s, 0, 0)),
            ],
            out_specs=[
                pl.BlockSpec((1, levels, row_total), lambda s, w: (s, 0, 0)),
                whole(senders, levels, width),
            ],
            scratch_shapes=[
                pltpu.VMEM((own, levels, lat_total), jnp.bfloat16),
                pltpu.VMEM((own, levels, lat_total), jnp.bfloat16),
            ],
        ),
        out_shape=[
            jax.ShapeDtypeStruct((own, levels, row_total), jnp.bfloat16),
            jax.ShapeDtypeStruct((senders, levels, width), jnp.bfloat16),
        ],
        compiler_params=pltpu.CompilerParams(vmem_limit_bytes=VMEM_LIMIT),
        cost_estimate=pl.CostEstimate(
            flops=8 * own * row_total * lat_total * levels,
            bytes_accessed=2 * own * row_total * lat_total,
            transcendentals=0,
        ),
        name="legendre",
    )(own_waves, counts, rates, to_t, from_t, rows, legendre)


def per_device(
    north_rows, south_rows, lon_counts, slot_wave, legendre, mode_rates, to_modes, from_modes
):
    lat_dev = north_rows.shape[0]
    slot_dev, row_total, lat_total = legendre.shape
    levels = to_modes.shape[0]
    my_index = lax.axis_index("wave")
    own_waves = lax.dynamic_slice_in_dim(slot_wave, my_index * slot_dev, slot_dev)
    local_counts = lax.dynamic_slice_in_dim(lon_counts, my_index * lat_dev, lat_dev)
    north = jnp.transpose(north_rows, (2, 0, 1))
    south = jnp.transpose(south_rows, (2, 0, 1))
    counts_here, waves_all = local_counts[:, None], slot_wave[None, :]
    counts_all, rates = lon_counts[None, :], mode_rates[:, None]
    to_t, from_t = to_modes.T, from_modes.T
    states, outs = [], []
    for part in range(2):
        rows = symmetric_part(part, levels, north, south, counts_here, waves_all)
        packed = pack(jnp.transpose(rows, (2, 0, 1)), slot_dev)
        moved = lax.all_to_all(packed, "wave", split_axis=0, concat_axis=0, tiled=True)
        state, back = compute(moved, legendre, own_waves, counts_all, rates, to_t, from_t)
        home = lax.all_to_all(back, "wave", split_axis=0, concat_axis=0, tiled=True)
        states.append(jnp.transpose(state, (1, 0, 2)))
        outs.append(jnp.transpose(unpack(home, slot_dev), (1, 2, 0)))
    spec_state = jnp.transpose(jnp.concatenate(states, axis=0), (1, 2, 0))
    new_rows = jnp.transpose(jnp.concatenate(outs, axis=0), (1, 2, 0))
    return (spec_state, new_rows)


def solution(mesh):
    in_specs = (
        P(("grp", "wave"), None, None),
        P(("grp", "wave"), None, None),
        P(),
        P(),
        P("wave", None, None),
        P(),
        P(),
        P(),
    )
    out_specs = (P(("grp", "wave"), None, None), P(("grp", "wave"), None, None))
    return jax.shard_map(
        per_device, mesh=mesh, in_specs=in_specs, out_specs=out_specs, check_vma=False
    )
```

time: 584 us -> 344 us (0.59)
  waiting for transfers between devices: 329 us -> 160 us
  local copies, waits for them, and re-layouts: 153 us -> 32.8 us
  Pallas kernels: 0 us -> 115 us
  matrix products: 59.3 us -> 0 us
  other arithmetic: 27.3 us -> 12.1 us
  starting transfers between devices: 11.4 us -> 20.8 us
    all_to_all x2 -> x4, waiting for transfers between devices: 329 us -> 160 us  [the longest x2 84.7 us: per_device(): home = lax.all_to_all(back, 'wave', split_axis=0, concat_axis=0, tiled=True)]
    pallas_call x0 -> x8, Pallas kernels: none -> 115 us  [the longest x2 56.9 us: compute(): pl.pallas_call(functools.partial(compute_kernel, own, senders, lats), gri...]
    dot_general x4 -> x0, matrix products: 59.3 us -> none  [the longest x1 25.7 us: per_device(): jnp.einsum('snj,jsc->snc', legendre, columns, preferred_element_type=jnp....]
    convert_element_type x3 -> x0, local copies, waits for them, and re-layouts: 39.9 us -> none  [the longest x1 25.2 us: vertical_step(): scaled = (modal_part / divisor).astype(jnp.bfloat16).reshape(-1, levels)]
    all_to_all x3 -> x0, local copies, waits for them, and re-layouts: 35.6 us -> none  [the longest x2 27.8 us: per_device(): lax.all_to_all(sym_here, 'wave', split_axis=1, concat_axis=0, tiled=True)]
    reshape x2 -> x0, local copies, waits for them, and re-layouts: 34.9 us -> none  [the longest x1 18.9 us: vertical_step(): scaled = (modal_part / divisor).astype(jnp.bfloat16).reshape(-1, levels)]
    unnamed x16 -> x18, local copies, waits for them, and re-layouts: 42.2 us -> 16.7 us
    convert_element_type x3 -> x0, other arithmetic: 23.7 us -> none  [the longest x1 9.62 us: per_device(): jnp.where(live_here[:, :, None], summed, 0.0).astype(jnp.bfloat16)]
  transfers between devices with their start and end apart: 2 -> 4, of which waited for: 2 -> 4; matrix products, arithmetic and copies ran while one was open for 2% -> 5% of each run, Pallas kernels for 0% -> 25%
where the time goes in v1:
time: 344 us; the launch traced here: 341 us
  waiting for transfers between devices  160 us (47%)
  Pallas kernels  115 us (33%)
  local copies, waits for them, and re-layouts  32.8 us (10%)
  starting transfers between devices  20.8 us (6%)
  other arithmetic  12.1 us (4%)
    all_to_all x2, waiting for transfers between devices, per_device(): home = lax.all_to_all(back, 'wave', split_axis=0, concat_axis=0, tiled=True)  84.7 us
    all_to_all x2, waiting for transfers between devices, per_device(): lax.all_to_all(packed, 'wave', split_axis=0, concat_axis=0, tiled=True)  75.5 us
    pallas_call x2, Pallas kernels, compute(): pl.pallas_call(functools.partial(compute_kernel, own, senders, lats), gri...  56.9 us
    pallas_call x2, Pallas kernels, pack(): pl.pallas_call(functools.partial(pack_kernel, own, lats), grid=(slots //...  22.7 us
    pallas_call x2, Pallas kernels, unpack(): pl.pallas_call(functools.partial(unpack_kernel, own, lats), grid=(senders...  22.5 us
    unnamed x18, local copies, waits for them, and re-layouts  16.7 us
    pallas_call x2, Pallas kernels, symmetric_part(): pl.pallas_call(sum_kernel, grid=(lats // step,), in_specs=[pl.BlockSpec((...  12.8 us
    pallas_call x2, local copies, waits for them, and re-layouts, symmetric_part(): pl.pallas_call(sum_kernel, grid=(lats // step,), in_specs=[pl.BlockSpec((...  12.6 us
  transfers between devices with their start and end apart: 4, of which 4 were waited for; matrix products, arithmetic and copies ran while one was open for 5% of the time, Pallas kernels for 25%

profile of v1, /device:TPU:13, one launch (start us, length us, event | category | flops | bytes accessed | tf_op | source)
XLA Modules:
  0.0 341.4 jit_solution(11739872456379047327)
XLA Ops:
  0.6 0.8 dynamic-slice_bitcast_fusion
  1.4 0.7 copy.20.counts_ref
  2.1 6.4 %sum0.1 = bf16[137,80,128]{2,1,0:T(8,128)(2,1)} custom-call(s32[80,1]{1,0:T(8,128)} %copy.20.counts_ref, s32[1,128]{1,0:T(1,128)} %bitcast.32, bf16[274,80,128]{2,1,0:T(8,128)(2,1)} %bitcast.18, bf16[274,80,128]{2,1,0:T(8,128)(2,1)} %bitcast.20), custom_call_target="tpu_custom_call" | custom-call | tf_op jit(solution)/shard_map/sum0/pallas_call | solution.py:23
  8.5 6.3 %copy.21 = bf16[137,80,128]{1,0,2:T(8,128)(2,1)} copy(bf16[137,80,128]{2,1,0:T(8,128)(2,1)} %sum0.1) | data formatting | bytes 5611520 | tf_op jit(solution)/shard_map/sum0/pallas_call | solution.py:23
  14.8 11.4 %pack.2 = bf16[16,137,640]{2,1,0:T(8,128)(2,1)} custom-call(bf16[128,137,80]{2,1,0:T(8,128)(2,1)} %bitcast.24), custom_call_target="tpu_custom_call" | custom-call | tf_op jit(solution)/shard_map/pack/pallas_call | solution.py:45
  26.2 6.5 %all-to-all-start = ((bf16[16,137,640]{2,1,0:T(8,128)(2,1)}), bf16[16,137,640]{2,1,0:T(8,128)(2,1)S(1)}, u32[]{:S(2)}, u32[]{:S(2)}) async-start(bf16[16,137,640]{2,1,0:T(8,128)(2,1)} %pack.2), calls=%async_computation | async-start | bytes 5898240 | tf_op jit(solution)/shard_map/all_to_all | solution.py:167
  32.7 6.4 %sum1.1 = bf16[137,80,128]{2,1,0:T(8,128)(2,1)} custom-call(s32[80,1]{1,0:T(8,128)} %copy.20.counts_ref, s32[1,128]{1,0:T(1,128)} %bitcast.33, bf16[274,80,128]{2,1,0:T(8,128)(2,1)} %bitcast.19, bf16[274,80,128]{2,1,0:T(8,128)(2,1)} %bitcast.21), custom_call_target="tpu_custom_call" | custom-call | tf_op jit(solution)/shard_map/sum1/pallas_call | solution.py:23
  39.1 6.3 %copy.24 = bf16[137,80,128]{1,0,2:T(8,128)(2,1)} copy(bf16[137,80,128]{2,1,0:T(8,128)(2,1)} %sum1.1) | data formatting | bytes 5611520 | tf_op jit(solution)/shard_map/sum1/pallas_call | solution.py:23
  45.4 11.4 %pack.3 = bf16[16,137,640]{2,1,0:T(8,128)(2,1)} custom-call(bf16[128,137,80]{2,1,0:T(8,128)(2,1)} %bitcast.25), custom_call_target="tpu_custom_call" | custom-call | tf_op jit(solution)/shard_map/pack/pallas_call | solution.py:45
  56.8 0.0 copy-start.4
  56.8 0.0 copy-start.5
  56.8 0.0 copy-start.6
  56.8 0.0 copy-start.2
  56.8 0.0 copy-start.3
  56.8 41.6 %all-to-all-done.rows_ref = bf16[16,137,640]{2,1,0:T(8,128)(2,1)S(1)} async-done(((bf16[16,137,640]{2,1,0:T(8,128)(2,1)}), bf16[16,137,640]{2,1,0:T(8,128)(2,1)S(1)}, u32[]{:S(2)}, u32[]{:S(2)}) %all-to-all-start) | async-done | bytes 2805792 | tf_op jit(solution)/shard_map/all_to_all | solution.py:167
  98.4 0.0 copy-start.1
  98.4 4.8 %all-to-all-start.1 = ((bf16[16,137,640]{2,1,0:T(8,128)(2,1)}), bf16[16,137,640]{2,1,0:T(8,128)(2,1)}, u32[]{:S(2)}, u32[]{:S(2)}) async-start(bf16[16,137,640]{2,1,0:T(8,128)(2,1)} %pack.3), calls=%async_computation.1 | async-start | bytes 5898240 | tf_op jit(solution)/shard_map/all_to_all | solution.py:167
  103.2 0.0 copy-done.4
  103.2 0.6 broadcast_in_dim.12.counts_ref
  103.8 0.0 copy-done.5
  103.8 0.6 dynamic_slice.6.waves_ref
  104.4 0.0 copy-done.6
  104.4 0.7 copy.22.rates_ref
  105.2 0.0 copy-done.2
  105.2 0.7 copy.18
  105.9 0.0 copy-done.3
  105.9 0.7 copy.19
  106.6 0.0 copy-done.1
  106.6 28.4 %legendre.2 = (bf16[8,137,1280]{2,1,0:T(8,128)(2,1)}, bf16[16,137,640]{2,1,0:T(8,128)(2,1)}) custom-call(s32[8]{0:T(128)} %dynamic_slice.6.waves_ref, s32[1,1280]{1,0:T(1,128)} %broadcast_in_dim.12.counts_ref, f32[137,1]{1,0:T(8,128)} %copy.22.rates_ref, bf16[137,137]{1,0:T(8,128)(2,1)} %bitcast.28, bf16[137,137]{1,0:T(8,128)(2,1)} %bitcast.30, ...), custom_call_target="tpu_custom_call" | custom-call | flops 14365491200 | bytes 26214400 | tf_op jit(solution)/shard_map/legendre/pallas_call | solution.py:113
  135.1 33.9 %all-to-all-done.1.rows_ref = bf16[16,137,640]{2,1,0:T(8,128)(2,1)} async-done(((bf16[16,137,640]{2,1,0:T(8,128)(2,1)}), bf16[16,137,640]{2,1,0:T(8,128)(2,1)}, u32[]{:S(2)}, u32[]{:S(2)}) %all-to-all-start.1) | async-done | bytes 2805792 | tf_op jit(solution)/shard_map/all_to_all | solution.py:167
  168.9 4.8 %all-to-all-start.2 = ((bf16[16,137,640]{2,1,0:T(8,128)(2,1)}), bf16[16,137,640]{2,1,0:T(8,128)(2,1)S(1)}, u32[]{:S(2)}, u32[]{:S(2)}) async-start(bf16[16,137,640]{2,1,0:T(8,128)(2,1)} %get-tuple-element.8), calls=%async_computation.2 | async-start | bytes 5898240 | tf_op jit(solution)/shard_map/all_to_all | solution.py:169
  173.7 28.4 %legendre.3 = (bf16[8,137,1280]{2,1,0:T(8,128)(2,1)}, bf16[16,137,640]{2,1,0:T(8,128)(2,1)}) custom-call(s32[8]{0:T(128)} %dynamic_slice.6.waves_ref, s32[1,1280]{1,0:T(1,128)} %broadcast_in_dim.12.counts_ref, f32[137,1]{1,0:T(8,128)} %copy.22.rates_ref, bf16[137,137]{1,0:T(8,128)(2,1)} %bitcast.29, bf16[137,137]{1,0:T(8,128)(2,1)} %bitcast.31, ...), custom_call_target="tpu_custom_call" | custom-call | flops 14365491200 | bytes 26214400 | tf_op jit(solution)/shard_map/legendre/pallas_call | solution.py:113
  202.1 37.3 %all-to-all-done.2.in_ref = bf16[16,137,640]{2,1,0:T(8,128)(2,1)S(1)} async-done(((bf16[16,137,640]{2,1,0:T(8,128)(2,1)}), bf16[16,137,640]{2,1,0:T(8,128)(2,1)S(1)}, u32[]{:S(2)}, u32[]{:S(2)}) %all-to-all-start.2) | async-done | bytes 2805792 | tf_op jit(solution)/shard_map/all_to_all | solution.py:169
  239.4 0.0 copy-start
  239.4 4.8 %all-to-all-start.3 = ((bf16[16,137,640]{2,1,0:T(8,128)(2,1)}), bf16[16,137,640]{2,1,0:T(8,128)(2,1)}, u32[]{:S(2)}, u32[]{:S(2)}) async-start(bf16[16,137,640]{2,1,0:T(8,128)(2,1)} %get-tuple-element.9), calls=%async_computation.3 | async-start | bytes 5898240 | tf_op jit(solution)/shard_map/all_to_all | solution.py:169
  244.2 3.5 %maximum_bitcast_fusion.1 = bf16[8,1280,274]{1,2,0:T(8,128)(2,1)S(1)} fusion(bf16[137,8,1280]{2,0,1:T(8,128)(2,1)} %bitcast.27, bf16[137,8,1280]{2,0,1:T(8,128)(2,1)} %bitcast.26), kind=kLoop, calls=%fused_computation.1 | loop fusion | flops 11223040 | bytes 11223040 | tf_op jit(solution)/shard_map/transpose | solution.py:172
  247.7 0.0 copy-done
  247.7 3.6 %copy.26 = bf16[8,1280,274]{1,0,2:T(8,128)(2,1)} copy(bf16[8,1280,274]{1,2,0:T(8,128)(2,1)S(1)} %maximum_bitcast_fusion.1) | data formatting | bytes 11223040
  251.3 11.2 %unpack.2 = bf16[128,137,80]{2,1,0:T(8,128)(2,1)} custom-call(bf16[16,137,640]{2,1,0:T(8,128)(2,1)} %copy-done), custom_call_target="tpu_custom_call" | custom-call | tf_op jit(solution)/shard_map/unpack/pallas_call | solution.py:63
  262.5 47.4 %all-to-all-done.3.in_ref = bf16[16,137,640]{2,1,0:T(8,128)(2,1)} async-done(((bf16[16,137,640]{2,1,0:T(8,128)(2,1)}), bf16[16,137,640]{2,1,0:T(8,128)(2,1)}, u32[]{:S(2)}, u32[]{:S(2)}) %all-to-all-start.3) | async-done | bytes 2805792 | tf_op jit(solution)/shard_map/all_to_all | solution.py:169
  310.0 11.3 %unpack.3 = bf16[128,137,80]{2,1,0:T(8,128)(2,1)} custom-call(bf16[16,137,640]{2,1,0:T(8,128)(2,1)} %all-to-all-done.3.in_ref), custom_call_target="tpu_custom_call" | custom-call | tf_op jit(solution)/shard_map/unpack/pallas_call | solution.py:63
  321.2 8.5 %maximum_bitcast_fusion = bf16[80,128,274]{0,2,1:T(8,128)(2,1)} fusion(bf16[137,80,128]{1,0,2:T(8,128)(2,1)} %bitcast.23, bf16[137,80,128]{1,0,2:T(8,128)(2,1)} %bitcast.22), kind=kLoop, calls=%fused_computation | loop fusion | flops 11223040 | bytes 11223040 | tf_op jit(solution)/shard_map/transpose | solution.py:173
  329.8 11.6 %copy.27 = bf16[80,128,274]{1,0,2:T(8,128)(2,1)} copy(bf16[80,128,274]{0,2,1:T(8,128)(2,1)} %maximum_bitcast_fusion) | data formatting | bytes 11223040
Async XLA Ops:
  26.2 72.2 %all-to-all-start = ((bf16[16,137,640]{2,1,0:T(8,128)(2,1)}), bf16[16,137,640]{2,1,0:T(8,128)(2,1)S(1)}, u32[]{:S(2)}, u32[]{:S(2)}) async-start(bf16[16,137,640]{2,1,0:T(8,128)(2,1)} %pack.2), calls=%async_computation | async-start | bytes 5898240 | tf_op jit(solution)/shard_map/all_to_all | solution.py:167
  56.8 46.4 %copy-start.4 = (s32[1280]{0:T(1024)S(1)}, s32[1280]{0:T(1024)}, u32[]{:S(2)}) copy-start(s32[1280]{0:T(1024)} %param.10) | copy-start | bytes 15364
  56.8 47.0 %copy-start.5 = (s32[128]{0:T(128)S(1)}, s32[128]{0:T(128)}, u32[]{:S(2)}) copy-start(s32[128]{0:T(128)} %param.11) | copy-start | bytes 1540
  56.8 47.6 %copy-start.6 = (f32[137]{0:T(256)S(1)}, f32[137]{0:T(256)}, u32[]{:S(2)}) copy-start(f32[137]{0:T(256)} %param.13) | copy-start | bytes 1648
  56.8 48.4 %copy-start.2 = (bf16[137,137]{1,0:T(8,128)(2,1)S(1)}, bf16[137,137]{1,0:T(8,128)(2,1)}, u32[]{:S(2)}) copy-start(bf16[137,137]{1,0:T(8,128)(2,1)} %param.14) | copy-start | bytes 112618
  56.8 49.1 %copy-start.3 = (bf16[137,137]{1,0:T(8,128)(2,1)S(1)}, bf16[137,137]{1,0:T(8,128)(2,1)}, u32[]{:S(2)}) copy-start(bf16[137,137]{1,0:T(8,128)(2,1)} %param.15) | copy-start | bytes 112618
  98.4 8.3 %copy-start.1 = (bf16[16,137,640]{2,1,0:T(8,128)(2,1)}, bf16[16,137,640]{2,1,0:T(8,128)(2,1)S(1)}, u32[]{:S(2)}) copy-start(bf16[16,137,640]{2,1,0:T(8,128)(2,1)S(1)} %all-to-all-done.rows_ref) | copy-start | bytes 8417284
  98.4 70.6 %all-to-all-start.1 = ((bf16[16,137,640]{2,1,0:T(8,128)(2,1)}), bf16[16,137,640]{2,1,0:T(8,128)(2,1)}, u32[]{:S(2)}, u32[]{:S(2)}) async-start(bf16[16,137,640]{2,1,0:T(8,128)(2,1)} %pack.3), calls=%async_computation.1 | async-start | bytes 5898240 | tf_op jit(solution)/shard_map/all_to_all | solution.py:167
  168.9 70.5 %all-to-all-start.2 = ((bf16[16,137,640]{2,1,0:T(8,128)(2,1)}), bf16[16,137,640]{2,1,0:T(8,128)(2,1)S(1)}, u32[]{:S(2)}, u32[]{:S(2)}) async-start(bf16[16,137,640]{2,1,0:T(8,128)(2,1)} %get-tuple-element.8), calls=%async_computation.2 | async-start | bytes 5898240 | tf_op jit(solution)/shard_map/all_to_all | solution.py:169
  239.4 8.3 %copy-start = (bf16[16,137,640]{2,1,0:T(8,128)(2,1)}, bf16[16,137,640]{2,1,0:T(8,128)(2,1)S(1)}, u32[]{:S(2)}) copy-start(bf16[16,137,640]{2,1,0:T(8,128)(2,1)S(1)} %all-to-all-done.2.in_ref) | copy-start | bytes 8417284
  239.4 70.6 %all-to-all-start.3 = ((bf16[16,137,640]{2,1,0:T(8,128)(2,1)}), bf16[16,137,640]{2,1,0:T(8,128)(2,1)}, u32[]{:S(2)}, u32[]{:S(2)}) async-start(bf16[16,137,640]{2,1,0:T(8,128)(2,1)} %get-tuple-element.9), calls=%async_computation.3 | async-start | bytes 5898240 | tf_op jit(solution)/shard_map/all_to_all | solution.py:169

commit v2 on v1

--- a/solution.py
+++ b/solution.py
@@ -9,65 +9,71 @@
 
 NMAX = 2559
 VMEM_LIMIT = 60 * 1024 * 1024
+STEP = 16
 
 
-def sum_kernel(counts_ref, waves_ref, north_ref, south_ref, out_ref):
+def pack_kernel(own, counts_ref, waves_ref, north_ref, south_ref, out_ref, turned):
+    lats = north_ref.shape[2]
     live = 2 * waves_ref[...] < counts_ref[...]
-    total = north_ref[...].astype(jnp.float32) + south_ref[...].astype(jnp.float32)
-    out_ref[...] = jnp.where(live[None], total, 0.0).astype(jnp.bfloat16)
+    total = north_ref[0].astype(jnp.float32) + south_ref[0].astype(jnp.float32)
+    turned[...] = jnp.swapaxes(jnp.where(live[None], total, 0.0), 1, 2)
+    for d in range(out_ref.shape[0]):
+        for i in range(own):
+            rows = turned[:, own * d + i, :].astype(jnp.bfloat16)
+            out_ref[d, :, lats * i : lats * (i + 1)] = rows
 
 
-def symmetric_part(part, levels, north, south, counts, waves):
-    _, lats, slots = north.shape
-    step = next((t for t in (16, 8) if lats % t == 0), lats)
+def pack(part, own, north, south, counts, waves):
+    _, levels, lats, slots = north.shape
+    rows = pl.BlockSpec((1, STEP, lats, slots), lambda g: (part, g, 0, 0))
     return pl.pallas_call(
-        sum_kernel,
-        grid=(lats // step,),
+        functools.partial(pack_kernel, own),
+        grid=(pl.cdiv(levels, STEP),),
         in_specs=[
-            pl.BlockSpec((step, 1), lambda g: (g, 0)),
+            pl.BlockSpec((lats, 1), lambda g: (0, 0)),
             pl.BlockSpec((1, slots), lambda g: (0, 0)),
-            pl.BlockSpec((levels, step, slots), lambda g: (part, g, 0)),
-            pl.BlockSpec((levels, step, slots), lambda g: (part, g, 0)),
+            rows,
+            rows,
         ],
-        out_specs=pl.BlockSpec((levels, step, slots), lambda g: (0, g, 0)),
-        out_shape=jax.ShapeDtypeStruct((levels, lats, slots), jnp.bfloat16),
-        name=f"sum{part}",
+        out_specs=pl.BlockSpec((slots // own, STEP, own * lats), lambda g: (0, g, 0)),
+        out_shape=jax.ShapeDtypeStruct((slots // own, levels, own * lats), jnp.bfloat16),
+        scratch_shapes=[pltpu.VMEM((STEP, slots, lats), jnp.float32)],
+        cost_estimate=pl.CostEstimate(flops=0, bytes_accessed=levels * lats * slots * 6, transcendentals=0),
+        name=f"pack{part}",
     )(counts, waves, north, south)
 
 
-def pack_kernel(own, lats, in_ref, out_ref):
-    for i in range(own):
-        out_ref[0, :, lats * i : lats * (i + 1)] = in_ref[i]
+def unpack_kernel(own, in_ref, *refs):
+    out_ref, turned = refs[-2:]
+    lats = out_ref.shape[2]
+    for d in range(in_ref.shape[0]):
+        for i in range(own):
+            rows = in_ref[d, :, lats * i : lats * (i + 1)]
+            turned[:, own * d + i, :] = rows.astype(jnp.float32)
+    out_ref[0] = jnp.swapaxes(turned[...], 1, 2).astype(jnp.bfloat16)
 
 
-def pack(rows, own):
-    slots, levels, lats = rows.shape
+def unpack(part, own, packed, placed):
+    senders, levels, width = packed.shape
+    lats, slots = width // own, senders * own
+    in_specs = [pl.BlockSpec((senders, STEP, width), lambda g: (0, g, 0))]
+    operands = [packed]
+    aliases = {}
+    if placed is not None:
+        in_specs.append(pl.BlockSpec(memory_space=pl.ANY))
+        operands.append(placed)
+        aliases = {1: 0}
     return pl.pallas_call(
-        functools.partial(pack_kernel, own, lats),
-        grid=(slots // own,),
-        in_specs=[pl.BlockSpec((own, levels, lats), lambda d: (d, 0, 0))],
-        out_specs=pl.BlockSpec((1, levels, own * lats), lambda d: (d, 0, 0)),
-        out_shape=jax.ShapeDtypeStruct((slots // own, levels, own * lats), jnp.bfloat16),
-        name="pack",
-    )(rows)
-
-
-def unpack_kernel(own, lats, in_ref, out_ref):
-    for i in range(own):
-        out_ref[i] = in_ref[0, :, lats * i : lats * (i + 1)]
-
-
-def unpack(packed, own):
-    senders, levels, width = packed.shape
-    lats = width // own
-    return pl.pallas_call(
-        functools.partial(unpack_kernel, own, lats),
-        grid=(senders,),
-        in_specs=[pl.BlockSpec((1, levels, width), lambda d: (d, 0, 0))],
-        out_specs=pl.BlockSpec((own, levels, lats), lambda d: (d, 0, 0)),
-        out_shape=jax.ShapeDtypeStruct((senders * own, levels, lats), jnp.bfloat16),
-        name="unpack",
-    )(packed)
+        functools.partial(unpack_kernel, own),
+        grid=(pl.cdiv(levels, STEP),),
+        in_specs=in_specs,
+        out_specs=pl.BlockSpec((1, STEP, lats, slots), lambda g: (part, g, 0, 0)),
+        out_shape=jax.ShapeDtypeStruct((2, levels, lats, slots), jnp.bfloat16),
+        scratch_shapes=[pltpu.VMEM((STEP, slots, lats), jnp.float32)],
+        input_output_aliases=aliases,
+        cost_estimate=pl.CostEstimate(flops=0, bytes_accessed=levels * lats * slots * 4, transcendentals=0),
+        name=f"unpack{part}",
+    )(*operands)
 
 
 def compute_kernel(
@@ -155,22 +161,22 @@
     my_index = lax.axis_index("wave")
     own_waves = lax.dynamic_slice_in_dim(slot_wave, my_index * slot_dev, slot_dev)
     local_counts = lax.dynamic_slice_in_dim(lon_counts, my_index * lat_dev, lat_dev)
-    north = jnp.transpose(north_rows, (2, 0, 1))
-    south = jnp.transpose(south_rows, (2, 0, 1))
+    slots = slot_wave.shape[0]
+    north = jnp.transpose(north_rows, (2, 0, 1)).reshape(2, levels, lat_dev, slots)
+    south = jnp.transpose(south_rows, (2, 0, 1)).reshape(2, levels, lat_dev, slots)
     counts_here, waves_all = local_counts[:, None], slot_wave[None, :]
     counts_all, rates = lon_counts[None, :], mode_rates[:, None]
     to_t, from_t = to_modes.T, from_modes.T
-    states, outs = [], []
+    states, placed = [], None
     for part in range(2):
-        rows = symmetric_part(part, levels, north, south, counts_here, waves_all)
-        packed = pack(jnp.transpose(rows, (2, 0, 1)), slot_dev)
+        packed = pack(part, slot_dev, north, south, counts_here, waves_all)
         moved = lax.all_to_all(packed, "wave", split_axis=0, concat_axis=0, tiled=True)
         state, back = compute(moved, legendre, own_waves, counts_all, rates, to_t, from_t)
         home = lax.all_to_all(back, "wave", split_axis=0, concat_axis=0, tiled=True)
         states.append(jnp.transpose(state, (1, 0, 2)))
-        outs.append(jnp.transpose(unpack(home, slot_dev), (1, 2, 0)))
+        placed = unpack(part, slot_dev, home, placed)
     spec_state = jnp.transpose(jnp.concatenate(states, axis=0), (1, 2, 0))
-    new_rows = jnp.transpose(jnp.concatenate(outs, axis=0), (1, 2, 0))
+    new_rows = jnp.transpose(placed.reshape(2 * levels, lat_dev, slots), (1, 2, 0))
     return (spec_state, new_rows)
 
 

time: 344 us -> 335 us (0.974)
  Pallas kernels: 115 us -> 149 us
  local copies, waits for them, and re-layouts: 32.8 us -> 11.7 us
  waiting for transfers between devices: 160 us -> 149 us
  other arithmetic: 12.1 us -> 3.53 us
    pallas_call x6 -> x4, Pallas kernels: 58 us -> 91.8 us  [the longest x2 61.1 us: unpack(): pl.pallas_call(functools.partial(unpack_kernel, own), grid=(pl.cdiv(level...]
    all_to_all x2, waiting for transfers between devices: 84.7 us -> 65.4 us  [per_device(): home = lax.all_to_all(back, 'wave', split_axis=0, concat_axis=0, tiled=True)]
    pallas_call x2 -> x0, local copies, waits for them, and re-layouts: 12.6 us -> none  [symmetric_part(): pl.pallas_call(sum_kernel, grid=(lats // step,), in_specs=[pl.BlockSpec((...]
    all_to_all x2, waiting for transfers between devices: 75.5 us -> 84 us  [per_device(): lax.all_to_all(packed, 'wave', split_axis=0, concat_axis=0, tiled=True)]
    transpose x1 -> x0, other arithmetic: 8.54 us -> none  [per_device(): new_rows = jnp.transpose(jnp.concatenate(outs, axis=0), (1, 2, 0))]
    unnamed x18 -> x19, local copies, waits for them, and re-layouts: 16.7 us -> 8.25 us
  transfers between devices with their start and end apart: 4 -> 4, of which waited for: 4 -> 4; matrix products, arithmetic and copies ran while one was open for 5% -> 3% of each run, Pallas kernels for 25% -> 31%
where the time goes in v2:
time: 335 us
  Pallas kernels  149 us (44%)
  waiting for transfers between devices  149 us (44%)
  starting transfers between devices  20.8 us (6%)
  local copies, waits for them, and re-layouts  11.7 us (3%)
  other arithmetic  3.53 us (1%)
    all_to_all x2, waiting for transfers between devices, per_device(): lax.all_to_all(packed, 'wave', split_axis=0, concat_axis=0, tiled=True)  84 us
    all_to_all x2, waiting for transfers between devices, per_device(): home = lax.all_to_all(back, 'wave', split_axis=0, concat_axis=0, tiled=True)  65.4 us
    pallas_call x2, Pallas kernels, unpack(): pl.pallas_call(functools.partial(unpack_kernel, own), grid=(pl.cdiv(level...  61.1 us
    pallas_call x2, Pallas kernels, compute(): pl.pallas_call(functools.partial(compute_kernel, own, senders, lats), gri...  56.9 us
    pallas_call x2, Pallas kernels, pack(): pl.pallas_call(functools.partial(pack_kernel, own), grid=(pl.cdiv(levels,...  30.6 us
    all_to_all x2, starting transfers between devices, per_device(): lax.all_to_all(packed, 'wave', split_axis=0, concat_axis=0, tiled=True)  11.3 us
    all_to_all x2, starting transfers between devices, per_device(): home = lax.all_to_all(back, 'wave', split_axis=0, concat_axis=0, tiled=True)  9.56 us
    unnamed x19, local copies, waits for them, and re-layouts  8.25 us
  transfers between devices with their start and end apart: 4, of which 4 were waited for; matrix products, arithmetic and copies ran while one was open for 3% of the time, Pallas kernels for 31%

profile of v2, /device:TPU:13, one launch (start us, length us, event | category | flops | bytes accessed | tf_op | source)
XLA Modules:
  0.0 334.9 jit_solution(12639425922800828534)
XLA Ops:
  0.6 0.8 dynamic-slice_bitcast_fusion
  1.4 0.7 copy.18.counts_ref
  2.1 15.3 %pack0.1 = bf16[16,137,640]{2,1,0:T(8,128)(2,1)} custom-call(s32[80,1]{1,0:T(8,128)} %copy.18.counts_ref, s32[1,128]{1,0:T(1,128)} %bitcast.30, bf16[2,137,80,128]{3,2,1,0:T(8,128)(2,1)} %bitcast.19, bf16[2,137,80,128]{3,2,1,0:T(8,128)(2,1)} %bitcast.21), custom_call_target="tpu_custom_call" | custom-call | bytes 8417280 | tf_op jit(solution)/shard_map/pack0/pallas_call | solution.py:29
  17.4 6.5 %all-to-all-start = ((bf16[16,137,640]{2,1,0:T(8,128)(2,1)}), bf16[16,137,640]{2,1,0:T(8,128)(2,1)S(1)}, u32[]{:S(2)}, u32[]{:S(2)}) async-start(bf16[16,137,640]{2,1,0:T(8,128)(2,1)} %pack0.1), calls=%async_computation | async-start | bytes 5898240 | tf_op jit(solution)/shard_map/all_to_all | solution.py:173
  23.9 15.3 %pack1.1 = bf16[16,137,640]{2,1,0:T(8,128)(2,1)} custom-call(s32[80,1]{1,0:T(8,128)} %copy.18.counts_ref, s32[1,128]{1,0:T(1,128)} %bitcast.31, bf16[2,137,80,128]{3,2,1,0:T(8,128)(2,1)} %bitcast.20, bf16[2,137,80,128]{3,2,1,0:T(8,128)(2,1)} %bitcast.22), custom_call_target="tpu_custom_call" | custom-call | bytes 8417280 | tf_op jit(solution)/shard_map/pack1/pallas_call | solution.py:29
  39.3 0.0 copy-start.5
  39.3 0.0 copy-start.6
  39.3 0.0 copy-start.7
  39.3 0.0 copy-start.3
  39.3 0.0 copy-start.4
  39.3 50.3 %all-to-all-done.rows_ref = bf16[16,137,640]{2,1,0:T(8,128)(2,1)S(1)} async-done(((bf16[16,137,640]{2,1,0:T(8,128)(2,1)}), bf16[16,137,640]{2,1,0:T(8,128)(2,1)S(1)}, u32[]{:S(2)}, u32[]{:S(2)}) %all-to-all-start) | async-done | bytes 2805792 | tf_op jit(solution)/shard_map/all_to_all | solution.py:173
  89.6 0.0 copy-start.2
  89.6 1.6 copy-done.2
  91.2 4.8 %all-to-all-start.1 = ((bf16[16,137,640]{2,1,0:T(8,128)(2,1)}), bf16[16,137,640]{2,1,0:T(8,128)(2,1)S(1)}, u32[]{:S(2)}, u32[]{:S(2)}) async-start(bf16[16,137,640]{2,1,0:T(8,128)(2,1)} %pack1.1), calls=%async_computation.1 | async-start | bytes 5898240 | tf_op jit(solution)/shard_map/all_to_all | solution.py:173
  96.0 0.0 copy-done.5
  96.0 0.6 broadcast_in_dim.12.counts_ref
  96.6 0.0 copy-done.6
  96.6 0.7 dynamic_slice.6.waves_ref
  97.2 0.0 copy-done.7
  97.3 0.8 copy.19.rates_ref
  98.0 0.0 copy-done.3
  98.0 0.7 copy.16
  98.7 0.0 copy-done.4
  98.7 0.7 copy.17
  99.5 28.5 %legendre.2 = (bf16[8,137,1280]{2,1,0:T(8,128)(2,1)}, bf16[16,137,640]{2,1,0:T(8,128)(2,1)}) custom-call(s32[8]{0:T(128)} %dynamic_slice.6.waves_ref, s32[1,1280]{1,0:T(1,128)} %broadcast_in_dim.12.counts_ref, f32[137,1]{1,0:T(8,128)} %copy.19.rates_ref, bf16[137,137]{1,0:T(8,128)(2,1)} %bitcast.26, bf16[137,137]{1,0:T(8,128)(2,1)} %bitcast.28, ...), custom_call_target="tpu_custom_call" | custom-call | flops 14365491200 | bytes 26214400 | tf_op jit(solution)/shard_map/legendre/pallas_call | solution.py:119
  128.0 33.7 %all-to-all-done.1.rows_ref = bf16[16,137,640]{2,1,0:T(8,128)(2,1)S(1)} async-done(((bf16[16,137,640]{2,1,0:T(8,128)(2,1)}), bf16[16,137,640]{2,1,0:T(8,128)(2,1)S(1)}, u32[]{:S(2)}, u32[]{:S(2)}) %all-to-all-start.1) | async-done | bytes 2805792 | tf_op jit(solution)/shard_map/all_to_all | solution.py:173
  161.7 0.0 copy-start.1
  161.7 1.6 copy-done.1
  163.3 4.8 %all-to-all-start.3 = ((bf16[16,137,640]{2,1,0:T(8,128)(2,1)}), bf16[16,137,640]{2,1,0:T(8,128)(2,1)S(1)}, u32[]{:S(2)}, u32[]{:S(2)}) async-start(bf16[16,137,640]{2,1,0:T(8,128)(2,1)} %get-tuple-element.9), calls=%async_computation.3 | async-start | bytes 5898240 | tf_op jit(solution)/shard_map/all_to_all | solution.py:175
  168.0 28.4 %legendre.3 = (bf16[8,137,1280]{2,1,0:T(8,128)(2,1)}, bf16[16,137,640]{2,1,0:T(8,128)(2,1)}) custom-call(s32[8]{0:T(128)} %dynamic_slice.6.waves_ref, s32[1,1280]{1,0:T(1,128)} %broadcast_in_dim.12.counts_ref, f32[137,1]{1,0:T(8,128)} %copy.19.rates_ref, bf16[137,137]{1,0:T(8,128)(2,1)} %bitcast.27, bf16[137,137]{1,0:T(8,128)(2,1)} %bitcast.29, ...), custom_call_target="tpu_custom_call" | custom-call | flops 14365491200 | bytes 26214400 | tf_op jit(solution)/shard_map/legendre/pallas_call | solution.py:119
  196.5 37.2 %all-to-all-done.3.in_ref = bf16[16,137,640]{2,1,0:T(8,128)(2,1)S(1)} async-done(((bf16[16,137,640]{2,1,0:T(8,128)(2,1)}), bf16[16,137,640]{2,1,0:T(8,128)(2,1)S(1)}, u32[]{:S(2)}, u32[]{:S(2)}) %all-to-all-start.3) | async-done | bytes 2805792 | tf_op jit(solution)/shard_map/all_to_all | solution.py:175
  233.7 0.0 copy-start
  233.7 4.8 %all-to-all-start.2 = ((bf16[16,137,640]{2,1,0:T(8,128)(2,1)}), bf16[16,137,640]{2,1,0:T(8,128)(2,1)}, u32[]{:S(2)}, u32[]{:S(2)}) async-start(bf16[16,137,640]{2,1,0:T(8,128)(2,1)} %get-tuple-element.8), calls=%async_computation.2 | async-start | bytes 5898240 | tf_op jit(solution)/shard_map/all_to_all | solution.py:175
  238.5 3.5 %maximum_bitcast_fusion = bf16[8,1280,274]{1,2,0:T(8,128)(2,1)S(1)} fusion(bf16[137,8,1280]{2,0,1:T(8,128)(2,1)} %bitcast.25, bf16[137,8,1280]{2,0,1:T(8,128)(2,1)} %bitcast.24), kind=kLoop, calls=%fused_computation | loop fusion | flops 11223040 | bytes 11223040 | tf_op jit(solution)/shard_map/transpose | solution.py:178
  242.0 0.0 copy-done
  242.0 3.6 %copy.22 = bf16[8,1280,274]{1,0,2:T(8,128)(2,1)} copy(bf16[8,1280,274]{1,2,0:T(8,128)(2,1)S(1)} %maximum_bitcast_fusion) | data formatting | bytes 11223040
  245.6 30.6 %unpack0.1.refs_0_ = bf16[2,137,80,128]{3,2,1,0:T(8,128)(2,1)} custom-call(bf16[16,137,640]{2,1,0:T(8,128)(2,1)} %copy-done), custom_call_target="tpu_custom_call" | custom-call | bytes 5611520 | tf_op jit(solution)/shard_map/unpack0/pallas_call | solution.py:66
  276.2 28.1 %all-to-all-done.2.in_ref = bf16[16,137,640]{2,1,0:T(8,128)(2,1)} async-done(((bf16[16,137,640]{2,1,0:T(8,128)(2,1)}), bf16[16,137,640]{2,1,0:T(8,128)(2,1)}, u32[]{:S(2)}, u32[]{:S(2)}) %all-to-all-start.2) | async-done | bytes 2805792 | tf_op jit(solution)/shard_map/all_to_all | solution.py:175
  304.3 30.6 %unpack1.1 = bf16[2,137,80,128]{3,2,1,0:T(8,128)(2,1)} custom-call(bf16[16,137,640]{2,1,0:T(8,128)(2,1)} %all-to-all-done.2.in_ref, bf16[2,137,80,128]{3,2,1,0:T(8,128)(2,1)} %unpack0.1.refs_0_), custom_call_target="tpu_custom_call", output_to_operand_aliasing={{}: (1, {})} | custom-call | bytes 5611520 | tf_op jit(solution)/shard_map/unpack1/pallas_call | solution.py:66
Async XLA Ops:
  17.4 72.2 %all-to-all-start = ((bf16[16,137,640]{2,1,0:T(8,128)(2,1)}), bf16[16,137,640]{2,1,0:T(8,128)(2,1)S(1)}, u32[]{:S(2)}, u32[]{:S(2)}) async-start(bf16[16,137,640]{2,1,0:T(8,128)(2,1)} %pack0.1), calls=%async_computation | async-start | bytes 5898240 | tf_op jit(solution)/shard_map/all_to_all | solution.py:173
  39.3 56.7 %copy-start.5 = (s32[1280]{0:T(1024)S(1)}, s32[1280]{0:T(1024)}, u32[]{:S(2)}) copy-start(s32[1280]{0:T(1024)} %param.10) | copy-start | bytes 15364
  39.3 57.3 %copy-start.6 = (s32[128]{0:T(128)S(1)}, s32[128]{0:T(128)}, u32[]{:S(2)}) copy-start(s32[128]{0:T(128)} %param.11) | copy-start | bytes 1540
  39.3 58.0 %copy-start.7 = (f32[137]{0:T(256)S(1)}, f32[137]{0:T(256)}, u32[]{:S(2)}) copy-start(f32[137]{0:T(256)} %param.13) | copy-start | bytes 1648
  39.3 58.7 %copy-start.3 = (bf16[137,137]{1,0:T(8,128)(2,1)S(1)}, bf16[137,137]{1,0:T(8,128)(2,1)}, u32[]{:S(2)}) copy-start(bf16[137,137]{1,0:T(8,128)(2,1)} %param.14) | copy-start | bytes 112618
  39.3 59.5 %copy-start.4 = (bf16[137,137]{1,0:T(8,128)(2,1)S(1)}, bf16[137,137]{1,0:T(8,128)(2,1)}, u32[]{:S(2)}) copy-start(bf16[137,137]{1,0:T(8,128)(2,1)} %param.15) | copy-start | bytes 112618
  89.6 1.6 copy-start.2
  91.2 70.5 %all-to-all-start.1 = ((bf16[16,137,640]{2,1,0:T(8,128)(2,1)}), bf16[16,137,640]{2,1,0:T(8,128)(2,1)S(1)}, u32[]{:S(2)}, u32[]{:S(2)}) async-start(bf16[16,137,640]{2,1,0:T(8,128)(2,1)} %pack1.1), calls=%async_computation.1 | async-start | bytes 5898240 | tf_op jit(solution)/shard_map/all_to_all | solution.py:173
  161.7 1.6 copy-start.1
  163.3 70.5 %all-to-all-start.3 = ((bf16[16,137,640]{2,1,0:T(8,128)(2,1)}), bf16[16,137,640]{2,1,0:T(8,128)(2,1)S(1)}, u32[]{:S(2)}, u32[]{:S(2)}) async-start(bf16[16,137,640]{2,1,0:T(8,128)(2,1)} %get-tuple-element.9), calls=%async_computation.3 | async-start | bytes 5898240 | tf_op jit(solution)/shard_map/all_to_all | solution.py:175
  233.7 8.3 %copy-start = (bf16[16,137,640]{2,1,0:T(8,128)(2,1)}, bf16[16,137,640]{2,1,0:T(8,128)(2,1)S(1)}, u32[]{:S(2)}) copy-start(bf16[16,137,640]{2,1,0:T(8,128)(2,1)S(1)} %all-to-all-done.3.in_ref) | copy-start | bytes 8417284
  233.7 70.6 %all-to-all-start.2 = ((bf16[16,137,640]{2,1,0:T(8,128)(2,1)}), bf16[16,137,640]{2,1,0:T(8,128)(2,1)}, u32[]{:S(2)}, u32[]{:S(2)}) async-start(bf16[16,137,640]{2,1,0:T(8,128)(2,1)} %get-tuple-element.8), calls=%async_computation.2 | async-start | bytes 5898240 | tf_op jit(solution)/shard_map/all_to_all | solution.py:175

commit v3 on v2

--- a/solution.py
+++ b/solution.py
@@ -10,13 +10,15 @@
 NMAX = 2559
 VMEM_LIMIT = 60 * 1024 * 1024
 STEP = 16
+UNPACK_STEP = 24
 
 
 def pack_kernel(own, counts_ref, waves_ref, north_ref, south_ref, out_ref, turned):
     lats = north_ref.shape[2]
     live = 2 * waves_ref[...] < counts_ref[...]
     total = north_ref[0].astype(jnp.float32) + south_ref[0].astype(jnp.float32)
-    turned[...] = jnp.swapaxes(jnp.where(live[None], total, 0.0), 1, 2)
+    kept = jnp.where(live[None], total, 0.0).astype(jnp.bfloat16)
+    turned[...] = jnp.swapaxes(kept, 1, 2).astype(jnp.float32)
     for d in range(out_ref.shape[0]):
         for i in range(own):
             rows = turned[:, own * d + i, :].astype(jnp.bfloat16)
@@ -49,14 +51,15 @@
     for d in range(in_ref.shape[0]):
         for i in range(own):
             rows = in_ref[d, :, lats * i : lats * (i + 1)]
-            turned[:, own * d + i, :] = rows.astype(jnp.float32)
-    out_ref[0] = jnp.swapaxes(turned[...], 1, 2).astype(jnp.bfloat16)
+            turned[own * d + i] = rows.astype(jnp.float32)
+    for c in range(out_ref.shape[1]):
+        out_ref[0, c] = turned[:, c, :].T.astype(jnp.bfloat16)
 
 
 def unpack(part, own, packed, placed):
     senders, levels, width = packed.shape
     lats, slots = width // own, senders * own
-    in_specs = [pl.BlockSpec((senders, STEP, width), lambda g: (0, g, 0))]
+    in_specs = [pl.BlockSpec((senders, UNPACK_STEP, width), lambda g: (0, g, 0))]
     operands = [packed]
     aliases = {}
     if placed is not None:
@@ -65,11 +68,11 @@
         aliases = {1: 0}
     return pl.pallas_call(
         functools.partial(unpack_kernel, own),
-        grid=(pl.cdiv(levels, STEP),),
+        grid=(pl.cdiv(levels, UNPACK_STEP),),
         in_specs=in_specs,
-        out_specs=pl.BlockSpec((1, STEP, lats, slots), lambda g: (part, g, 0, 0)),
+        out_specs=pl.BlockSpec((1, UNPACK_STEP, lats, slots), lambda g: (part, g, 0, 0)),
         out_shape=jax.ShapeDtypeStruct((2, levels, lats, slots), jnp.bfloat16),
-        scratch_shapes=[pltpu.VMEM((STEP, slots, lats), jnp.float32)],
+        scratch_shapes=[pltpu.VMEM((slots, UNPACK_STEP, lats), jnp.float32)],
         input_output_aliases=aliases,
         cost_estimate=pl.CostEstimate(flops=0, bytes_accessed=levels * lats * slots * 4, transcendentals=0),
         name=f"unpack{part}",

time: 335 us -> 313 us (0.934)
  Pallas kernels: 149 us -> 103 us
  waiting for transfers between devices: 149 us -> 172 us
    pallas_call x2, Pallas kernels: 61.1 us -> 17.9 us  [unpack(): pl.pallas_call(functools.partial(unpack_kernel, own), grid=(pl.cdiv(level...]
    all_to_all x2, waiting for transfers between devices: 65.4 us -> 87 us  [per_device(): home = lax.all_to_all(back, 'wave', split_axis=0, concat_axis=0, tiled=True)]
  transfers between devices with their start and end apart: 4 -> 4, of which waited for: 4 -> 4; matrix products, arithmetic and copies ran while one was open for 3% -> 3% of each run, Pallas kernels for 31% -> 26%
where the time goes in v3:
time: 313 us; the launch traced here: 312 us
  waiting for transfers between devices  172 us (55%)
  Pallas kernels  103 us (33%)
  starting transfers between devices  20.8 us (7%)
  local copies, waits for them, and re-layouts  11.7 us (4%)
  other arithmetic  3.53 us (1%)
    all_to_all x2, waiting for transfers between devices, per_device(): home = lax.all_to_all(back, 'wave', split_axis=0, concat_axis=0, tiled=True)  87 us
    all_to_all x2, waiting for transfers between devices, per_device(): lax.all_to_all(packed, 'wave', split_axis=0, concat_axis=0, tiled=True)  85.3 us
    pallas_call x2, Pallas kernels, compute(): pl.pallas_call(functools.partial(compute_kernel, own, senders, lats), gri...  56.9 us
    pallas_call x2, Pallas kernels, pack(): pl.pallas_call(functools.partial(pack_kernel, own), grid=(pl.cdiv(levels,...  28.1 us
    pallas_call x2, Pallas kernels, unpack(): pl.pallas_call(functools.partial(unpack_kernel, own), grid=(pl.cdiv(level...  17.9 us
    all_to_all x2, starting transfers between devices, per_device(): lax.all_to_all(packed, 'wave', split_axis=0, concat_axis=0, tiled=True)  11.3 us
    all_to_all x2, starting transfers between devices, per_device(): home = lax.all_to_all(back, 'wave', split_axis=0, concat_axis=0, tiled=True)  9.56 us
    unnamed x19, local copies, waits for them, and re-layouts  8.25 us
  transfers between devices with their start and end apart: 4, of which 4 were waited for; matrix products, arithmetic and copies ran while one was open for 3% of the time, Pallas kernels for 26%

profile of v3, /device:TPU:13, one launch (start us, length us, event | category | flops | bytes accessed | tf_op | source)
XLA Modules:
  0.0 312.0 jit_solution(13481593149944073337)
XLA Ops:
  0.6 0.8 dynamic-slice_bitcast_fusion
  1.4 0.7 copy.18.counts_ref
  2.1 14.0 %pack0.1 = bf16[16,137,640]{2,1,0:T(8,128)(2,1)} custom-call(s32[80,1]{1,0:T(8,128)} %copy.18.counts_ref, s32[1,128]{1,0:T(1,128)} %bitcast.30, bf16[2,137,80,128]{3,2,1,0:T(8,128)(2,1)} %bitcast.19, bf16[2,137,80,128]{3,2,1,0:T(8,128)(2,1)} %bitcast.21), custom_call_target="tpu_custom_call" | custom-call | bytes 8417280 | tf_op jit(solution)/shard_map/pack0/pallas_call | solution.py:31
  16.2 6.5 %all-to-all-start = ((bf16[16,137,640]{2,1,0:T(8,128)(2,1)}), bf16[16,137,640]{2,1,0:T(8,128)(2,1)S(1)}, u32[]{:S(2)}, u32[]{:S(2)}) async-start(bf16[16,137,640]{2,1,0:T(8,128)(2,1)} %pack0.1), calls=%async_computation | async-start | bytes 5898240 | tf_op jit(solution)/shard_map/all_to_all | solution.py:176
  22.7 14.1 %pack1.1 = bf16[16,137,640]{2,1,0:T(8,128)(2,1)} custom-call(s32[80,1]{1,0:T(8,128)} %copy.18.counts_ref, s32[1,128]{1,0:T(1,128)} %bitcast.31, bf16[2,137,80,128]{3,2,1,0:T(8,128)(2,1)} %bitcast.20, bf16[2,137,80,128]{3,2,1,0:T(8,128)(2,1)} %bitcast.22), custom_call_target="tpu_custom_call" | custom-call | bytes 8417280 | tf_op jit(solution)/shard_map/pack1/pallas_call | solution.py:31
  36.8 0.0 copy-start.5
  36.8 0.0 copy-start.6
  36.8 0.0 copy-start.7
  36.8 0.0 copy-start.3
  36.8 0.0 copy-start.4
  36.8 51.6 %all-to-all-done.rows_ref = bf16[16,137,640]{2,1,0:T(8,128)(2,1)S(1)} async-done(((bf16[16,137,640]{2,1,0:T(8,128)(2,1)}), bf16[16,137,640]{2,1,0:T(8,128)(2,1)S(1)}, u32[]{:S(2)}, u32[]{:S(2)}) %all-to-all-start) | async-done | bytes 2805792 | tf_op jit(solution)/shard_map/all_to_all | solution.py:176
  88.4 0.0 copy-start.2
  88.4 1.6 copy-done.2
  90.0 4.8 %all-to-all-start.1 = ((bf16[16,137,640]{2,1,0:T(8,128)(2,1)}), bf16[16,137,640]{2,1,0:T(8,128)(2,1)S(1)}, u32[]{:S(2)}, u32[]{:S(2)}) async-start(bf16[16,137,640]{2,1,0:T(8,128)(2,1)} %pack1.1), calls=%async_computation.1 | async-start | bytes 5898240 | tf_op jit(solution)/shard_map/all_to_all | solution.py:176
  94.7 0.0 copy-done.5
  94.7 0.6 broadcast_in_dim.12.counts_ref
  95.3 0.0 copy-done.6
  95.3 0.7 dynamic_slice.6.waves_ref
  96.0 0.0 copy-done.7
  96.0 0.8 copy.19.rates_ref
  96.8 0.0 copy-done.3
  96.8 0.7 copy.16
  97.5 0.0 copy-done.4
  97.5 0.7 copy.17
  98.2 28.5 %legendre.2 = (bf16[8,137,1280]{2,1,0:T(8,128)(2,1)}, bf16[16,137,640]{2,1,0:T(8,128)(2,1)}) custom-call(s32[8]{0:T(128)} %dynamic_slice.6.waves_ref, s32[1,1280]{1,0:T(1,128)} %broadcast_in_dim.12.counts_ref, f32[137,1]{1,0:T(8,128)} %copy.19.rates_ref, bf16[137,137]{1,0:T(8,128)(2,1)} %bitcast.26, bf16[137,137]{1,0:T(8,128)(2,1)} %bitcast.28, ...), custom_call_target="tpu_custom_call" | custom-call | flops 14365491200 | bytes 26214400 | tf_op jit(solution)/shard_map/legendre/pallas_call | solution.py:122
  126.7 33.7 %all-to-all-done.1.rows_ref = bf16[16,137,640]{2,1,0:T(8,128)(2,1)S(1)} async-done(((bf16[16,137,640]{2,1,0:T(8,128)(2,1)}), bf16[16,137,640]{2,1,0:T(8,128)(2,1)S(1)}, u32[]{:S(2)}, u32[]{:S(2)}) %all-to-all-start.1) | async-done | bytes 2805792 | tf_op jit(solution)/shard_map/all_to_all | solution.py:176
  160.4 0.0 copy-start.1
  160.4 1.6 copy-done.1
  162.0 4.8 %all-to-all-start.3 = ((bf16[16,137,640]{2,1,0:T(8,128)(2,1)}), bf16[16,137,640]{2,1,0:T(8,128)(2,1)S(1)}, u32[]{:S(2)}, u32[]{:S(2)}) async-start(bf16[16,137,640]{2,1,0:T(8,128)(2,1)} %get-tuple-element.9), calls=%async_computation.3 | async-start | bytes 5898240 | tf_op jit(solution)/shard_map/all_to_all | solution.py:178
  166.8 28.4 %legendre.3 = (bf16[8,137,1280]{2,1,0:T(8,128)(2,1)}, bf16[16,137,640]{2,1,0:T(8,128)(2,1)}) custom-call(s32[8]{0:T(128)} %dynamic_slice.6.waves_ref, s32[1,1280]{1,0:T(1,128)} %broadcast_in_dim.12.counts_ref, f32[137,1]{1,0:T(8,128)} %copy.19.rates_ref, bf16[137,137]{1,0:T(8,128)(2,1)} %bitcast.27, bf16[137,137]{1,0:T(8,128)(2,1)} %bitcast.29, ...), custom_call_target="tpu_custom_call" | custom-call | flops 14365491200 | bytes 26214400 | tf_op jit(solution)/shard_map/legendre/pallas_call | solution.py:122
  195.2 37.2 %all-to-all-done.3.in_ref = bf16[16,137,640]{2,1,0:T(8,128)(2,1)S(1)} async-done(((bf16[16,137,640]{2,1,0:T(8,128)(2,1)}), bf16[16,137,640]{2,1,0:T(8,128)(2,1)S(1)}, u32[]{:S(2)}, u32[]{:S(2)}) %all-to-all-start.3) | async-done | bytes 2805792 | tf_op jit(solution)/shard_map/all_to_all | solution.py:178
  232.5 0.0 copy-start
  232.5 4.8 %all-to-all-start.2 = ((bf16[16,137,640]{2,1,0:T(8,128)(2,1)}), bf16[16,137,640]{2,1,0:T(8,128)(2,1)}, u32[]{:S(2)}, u32[]{:S(2)}) async-start(bf16[16,137,640]{2,1,0:T(8,128)(2,1)} %get-tuple-element.8), calls=%async_computation.2 | async-start | bytes 5898240 | tf_op jit(solution)/shard_map/all_to_all | solution.py:178
  237.3 3.5 %maximum_bitcast_fusion = bf16[8,1280,274]{1,2,0:T(8,128)(2,1)S(1)} fusion(bf16[137,8,1280]{2,0,1:T(8,128)(2,1)} %bitcast.25, bf16[137,8,1280]{2,0,1:T(8,128)(2,1)} %bitcast.24), kind=kLoop, calls=%fused_computation | loop fusion | flops 11223040 | bytes 11223040 | tf_op jit(solution)/shard_map/transpose | solution.py:181
  240.8 0.0 copy-done
  240.8 3.6 %copy.22 = bf16[8,1280,274]{1,0,2:T(8,128)(2,1)} copy(bf16[8,1280,274]{1,2,0:T(8,128)(2,1)S(1)} %maximum_bitcast_fusion) | data formatting | bytes 11223040
  244.3 8.9 %unpack0.1.refs_0_ = bf16[2,137,80,128]{3,2,1,0:T(8,128)(2,1)} custom-call(bf16[16,137,640]{2,1,0:T(8,128)(2,1)} %copy-done), custom_call_target="tpu_custom_call" | custom-call | bytes 5611520 | tf_op jit(solution)/shard_map/unpack0/pallas_call | solution.py:69
  253.3 49.8 %all-to-all-done.2.in_ref = bf16[16,137,640]{2,1,0:T(8,128)(2,1)} async-done(((bf16[16,137,640]{2,1,0:T(8,128)(2,1)}), bf16[16,137,640]{2,1,0:T(8,128)(2,1)}, u32[]{:S(2)}, u32[]{:S(2)}) %all-to-all-start.2) | async-done | bytes 2805792 | tf_op jit(solution)/shard_map/all_to_all | solution.py:178
  303.0 8.9 %unpack1.1 = bf16[2,137,80,128]{3,2,1,0:T(8,128)(2,1)} custom-call(bf16[16,137,640]{2,1,0:T(8,128)(2,1)} %all-to-all-done.2.in_ref, bf16[2,137,80,128]{3,2,1,0:T(8,128)(2,1)} %unpack0.1.refs_0_), custom_call_target="tpu_custom_call", output_to_operand_aliasing={{}: (1, {})} | custom-call | bytes 5611520 | tf_op jit(solution)/shard_map/unpack1/pallas_call | solution.py:69
Async XLA Ops:
  16.2 72.2 %all-to-all-start = ((bf16[16,137,640]{2,1,0:T(8,128)(2,1)}), bf16[16,137,640]{2,1,0:T(8,128)(2,1)S(1)}, u32[]{:S(2)}, u32[]{:S(2)}) async-start(bf16[16,137,640]{2,1,0:T(8,128)(2,1)} %pack0.1), calls=%async_computation | async-start | bytes 5898240 | tf_op jit(solution)/shard_map/all_to_all | solution.py:176
  36.8 58.0 %copy-start.5 = (s32[1280]{0:T(1024)S(1)}, s32[1280]{0:T(1024)}, u32[]{:S(2)}) copy-start(s32[1280]{0:T(1024)} %param.10) | copy-start | bytes 15364
  36.8 58.6 %copy-start.6 = (s32[128]{0:T(128)S(1)}, s32[128]{0:T(128)}, u32[]{:S(2)}) copy-start(s32[128]{0:T(128)} %param.11) | copy-start | bytes 1540
  36.8 59.2 %copy-start.7 = (f32[137]{0:T(256)S(1)}, f32[137]{0:T(256)}, u32[]{:S(2)}) copy-start(f32[137]{0:T(256)} %param.13) | copy-start | bytes 1648
  36.8 60.0 %copy-start.3 = (bf16[137,137]{1,0:T(8,128)(2,1)S(1)}, bf16[137,137]{1,0:T(8,128)(2,1)}, u32[]{:S(2)}) copy-start(bf16[137,137]{1,0:T(8,128)(2,1)} %param.14) | copy-start | bytes 112618
  36.8 60.7 %copy-start.4 = (bf16[137,137]{1,0:T(8,128)(2,1)S(1)}, bf16[137,137]{1,0:T(8,128)(2,1)}, u32[]{:S(2)}) copy-start(bf16[137,137]{1,0:T(8,128)(2,1)} %param.15) | copy-start | bytes 112618
  88.4 1.6 copy-start.2
  90.0 70.5 %all-to-all-start.1 = ((bf16[16,137,640]{2,1,0:T(8,128)(2,1)}), bf16[16,137,640]{2,1,0:T(8,128)(2,1)S(1)}, u32[]{:S(2)}, u32[]{:S(2)}) async-start(bf16[16,137,640]{2,1,0:T(8,128)(2,1)} %pack1.1), calls=%async_computation.1 | async-start | bytes 5898240 | tf_op jit(solution)/shard_map/all_to_all | solution.py:176
  160.4 1.6 copy-start.1
  162.0 70.5 %all-to-all-start.3 = ((bf16[16,137,640]{2,1,0:T(8,128)(2,1)}), bf16[16,137,640]{2,1,0:T(8,128)(2,1)S(1)}, u32[]{:S(2)}, u32[]{:S(2)}) async-start(bf16[16,137,640]{2,1,0:T(8,128)(2,1)} %get-tuple-element.9), calls=%async_computation.3 | async-start | bytes 5898240 | tf_op jit(solution)/shard_map/all_to_all | solution.py:178
  232.5 8.3 %copy-start = (bf16[16,137,640]{2,1,0:T(8,128)(2,1)}, bf16[16,137,640]{2,1,0:T(8,128)(2,1)S(1)}, u32[]{:S(2)}) copy-start(bf16[16,137,640]{2,1,0:T(8,128)(2,1)S(1)} %all-to-all-done.3.in_ref) | copy-start | bytes 8417284
  232.5 70.6 %all-to-all-start.2 = ((bf16[16,137,640]{2,1,0:T(8,128)(2,1)}), bf16[16,137,640]{2,1,0:T(8,128)(2,1)}, u32[]{:S(2)}, u32[]{:S(2)}) async-start(bf16[16,137,640]{2,1,0:T(8,128)(2,1)} %get-tuple-element.8), calls=%async_computation.2 | async-start | bytes 5898240 | tf_op jit(solution)/shard_map/all_to_all | solution.py:178

commit v4 on v3

--- a/solution.py
+++ b/solution.py
@@ -14,9 +14,9 @@
 
 
 def pack_kernel(own, counts_ref, waves_ref, north_ref, south_ref, out_ref, turned):
-    lats = north_ref.shape[2]
+    lats = north_ref.shape[1]
     live = 2 * waves_ref[...] < counts_ref[...]
-    total = north_ref[0].astype(jnp.float32) + south_ref[0].astype(jnp.float32)
+    total = north_ref[...].astype(jnp.float32) + south_ref[...].astype(jnp.float32)
     kept = jnp.where(live[None], total, 0.0).astype(jnp.bfloat16)
     turned[...] = jnp.swapaxes(kept, 1, 2).astype(jnp.float32)
     for d in range(out_ref.shape[0]):
@@ -25,9 +25,10 @@
             out_ref[d, :, lats * i : lats * (i + 1)] = rows
 
 
-def pack(part, own, north, south, counts, waves):
-    _, levels, lats, slots = north.shape
-    rows = pl.BlockSpec((1, STEP, lats, slots), lambda g: (part, g, 0, 0))
+def pack(part, own, first, levels, north, south, counts, waves):
+    _, lats, slots = north.shape
+    start = first // STEP
+    rows = pl.BlockSpec((STEP, lats, slots), lambda g: (start + g, 0, 0))
     return pl.pallas_call(
         functools.partial(pack_kernel, own),
         grid=(pl.cdiv(levels, STEP),),
@@ -80,16 +81,22 @@
 
 
 def compute_kernel(
-    own, senders, lats, waves_ref, counts_ref, rates_ref, to_ref, from_ref, rows_ref, leg_ref,
-    state_ref, back_ref, columns, returned,
+    own, senders, lats, takes, waves_ref, counts_ref, rates_ref, to_ref, from_ref, leg_ref,
+    *refs,
 ):
+    *pieces, state_ref, back_ref, columns, returned = refs
     slot = pl.program_id(0)
 
     @pl.when(slot == 0)
     def _():
         for s in range(own):
             for d in range(senders):
-                columns[s, :, lats * d : lats * (d + 1)] = rows_ref[d, :, lats * s : lats * (s + 1)]
+                lanes = slice(lats * d, lats * (d + 1))
+                done = 0
+                for (skip, count), rows_ref in zip(takes, pieces):
+                    piece = rows_ref[d, skip : skip + count, lats * s : lats * (s + 1)]
+                    columns[s, done : done + count, lanes] = piece
+                    done += count
 
     wave = waves_ref[slot]
     direct = lax.dot_general(
@@ -114,13 +121,14 @@
                 back_ref[d, :, lats * s : lats * (s + 1)] = returned[s, :, lats * d : lats * (d + 1)]
 
 
-def compute(rows, legendre, own_waves, counts, rates, to_t, from_t):
-    senders, levels, width = rows.shape
+def compute(rows, takes, legendre, own_waves, counts, rates, to_t, from_t):
+    senders, _, width = rows[0].shape
+    levels = to_t.shape[0]
     own, row_total, lat_total = legendre.shape
     lats = lat_total // senders
     whole = lambda *shape: pl.BlockSpec(shape, lambda s, w: (0,) * len(shape))
     return pl.pallas_call(
-        functools.partial(compute_kernel, own, senders, lats),
+        functools.partial(compute_kernel, own, senders, lats, takes),
         grid_spec=pltpu.PrefetchScalarGridSpec(
             num_scalar_prefetch=1,
             grid=(own,),
@@ -129,8 +137,8 @@
                 whole(levels, 1),
                 whole(levels, levels),
                 whole(levels, levels),
-                whole(senders, levels, width),
                 pl.BlockSpec((1, row_total, lat_total), lambda s, w: (s, 0, 0)),
+                *[whole(*piece.shape) for piece in rows],
             ],
             out_specs=[
                 pl.BlockSpec((1, levels, row_total), lambda s, w: (s, 0, 0)),
@@ -152,7 +160,7 @@
             transcendentals=0,
         ),
         name="legendre",
-    )(own_waves, counts, rates, to_t, from_t, rows, legendre)
+    )(own_waves, counts, rates, to_t, from_t, legendre, *rows)
 
 
 def per_device(
@@ -165,16 +173,24 @@
     own_waves = lax.dynamic_slice_in_dim(slot_wave, my_index * slot_dev, slot_dev)
     local_counts = lax.dynamic_slice_in_dim(lon_counts, my_index * lat_dev, lat_dev)
     slots = slot_wave.shape[0]
-    north = jnp.transpose(north_rows, (2, 0, 1)).reshape(2, levels, lat_dev, slots)
-    south = jnp.transpose(south_rows, (2, 0, 1)).reshape(2, levels, lat_dev, slots)
+    north = jnp.transpose(north_rows, (2, 0, 1))
+    south = jnp.transpose(south_rows, (2, 0, 1))
     counts_here, waves_all = local_counts[:, None], slot_wave[None, :]
     counts_all, rates = lon_counts[None, :], mode_rates[:, None]
     to_t, from_t = to_modes.T, from_modes.T
-    states, placed = [], None
-    for part in range(2):
-        packed = pack(part, slot_dev, north, south, counts_here, waves_all)
-        moved = lax.all_to_all(packed, "wave", split_axis=0, concat_axis=0, tiled=True)
-        state, back = compute(moved, legendre, own_waves, counts_all, rates, to_t, from_t)
+    head = pl.cdiv(levels, STEP) * STEP
+    moved, states, placed = [], [], None
+    for part, (first, count) in enumerate(((0, head), (head, 2 * levels - head))):
+        packed = pack(part, slot_dev, first, count, north, south, counts_here, waves_all)
+        moved.append(lax.all_to_all(packed, "wave", split_axis=0, concat_axis=0, tiled=True))
+    cuts = (
+        (moved[:1], ((0, levels),)),
+        (moved, ((levels, head - levels), (0, 2 * levels - head))),
+    )
+    for part, (rows, takes) in enumerate(cuts):
+        state, back = compute(
+            rows, takes, legendre, own_waves, counts_all, rates, to_t, from_t
+        )
         home = lax.all_to_all(back, "wave", split_axis=0, concat_axis=0, tiled=True)
         states.append(jnp.transpose(state, (1, 0, 2)))
         placed = unpack(part, slot_dev, home, placed)

time: 313 us -> 306 us (0.978)
  waiting for transfers between devices: 172 us -> 167 us
  local copies, waits for them, and re-layouts: 11.7 us -> 8.52 us
    all_to_all x2, waiting for transfers between devices: 85.3 us -> 81.9 us  [per_device(): lax.all_to_all(packed, 'wave', split_axis=0, concat_axis=0, tiled=True)]
    unnamed x19 -> x17, local copies, waits for them, and re-layouts: 8.25 us -> 5.04 us
  transfers between devices with their start and end apart: 4 -> 4, of which waited for: 4 -> 4; matrix products, arithmetic and copies ran while one was open for 3% -> 3% of each run, Pallas kernels for 26% -> 27%
where the time goes in v4:
time: 306 us; the launch traced here: 305 us
  waiting for transfers between devices  167 us (55%)
  Pallas kernels  105 us (34%)
  starting transfers between devices  20.8 us (7%)
  local copies, waits for them, and re-layouts  8.52 us (3%)
  other arithmetic  3.53 us (1%)
    all_to_all x2, waiting for transfers between devices, per_device(): home = lax.all_to_all(back, 'wave', split_axis=0, concat_axis=0, tiled=True)  85.3 us
    all_to_all x2, waiting for transfers between devices, per_device(): lax.all_to_all(packed, 'wave', split_axis=0, concat_axis=0, tiled=True)  81.9 us
    pallas_call x2, Pallas kernels, compute(): pl.pallas_call(functools.partial(compute_kernel, own, senders, lats, take...  58.6 us
    pallas_call x2, Pallas kernels, pack(): pl.pallas_call(functools.partial(pack_kernel, own), grid=(pl.cdiv(levels,...  28.2 us
    pallas_call x2, Pallas kernels, unpack(): pl.pallas_call(functools.partial(unpack_kernel, own), grid=(pl.cdiv(level...  17.9 us
    all_to_all x2, starting transfers between devices, per_device(): lax.all_to_all(packed, 'wave', split_axis=0, concat_axis=0, tiled=True)  11.3 us
    all_to_all x2, starting transfers between devices, per_device(): home = lax.all_to_all(back, 'wave', split_axis=0, concat_axis=0, tiled=True)  9.56 us
  transfers between devices with their start and end apart: 4, of which 4 were waited for; matrix products, arithmetic and copies ran while one was open for 3% of the time, Pallas kernels for 27%

profile of v4, /device:TPU:13, one launch (start us, length us, event | category | flops | bytes accessed | tf_op | source)
XLA Modules:
  0.0 305.4 jit_solution(8370832150827818945)
XLA Ops:
  0.6 0.8 dynamic-slice_bitcast_fusion
  1.4 0.7 copy.18.counts_ref
  2.1 14.0 %pack0.1 = bf16[16,144,640]{2,1,0:T(8,128)(2,1)} custom-call(s32[80,1]{1,0:T(8,128)} %copy.18.counts_ref, s32[1,128]{1,0:T(1,128)} %bitcast.26, bf16[274,80,128]{2,1,0:T(8,128)(2,1)} %bitcast.15, bf16[274,80,128]{2,1,0:T(8,128)(2,1)} %bitcast.17), custom_call_target="tpu_custom_call" | custom-call | bytes 8847360 | tf_op jit(solution)/shard_map/pack0/pallas_call | solution.py:32
  16.2 6.5 %all-to-all-start = ((bf16[16,144,640]{2,1,0:T(8,128)(2,1)}), bf16[16,144,640]{2,1,0:T(8,128)(2,1)S(1)}, u32[]{:S(2)}, u32[]{:S(2)}) async-start(bf16[16,144,640]{2,1,0:T(8,128)(2,1)} %pack0.1), calls=%async_computation | async-start | bytes 5898240 | tf_op jit(solution)/shard_map/all_to_all | solution.py:185
  22.7 0.0 copy-start.4
  22.7 0.0 copy-start.5
  22.7 0.0 copy-start.6
  22.7 14.1 %pack1.1 = bf16[16,130,640]{2,1,0:T(8,128)(2,1)} custom-call(s32[80,1]{1,0:T(8,128)} %copy.18.counts_ref, s32[1,128]{1,0:T(1,128)} %bitcast.27, bf16[274,80,128]{2,1,0:T(8,128)(2,1)} %bitcast.16, bf16[274,80,128]{2,1,0:T(8,128)(2,1)} %bitcast.18), custom_call_target="tpu_custom_call" | custom-call | bytes 7987200 | tf_op jit(solution)/shard_map/pack1/pallas_call | solution.py:32
  36.8 0.0 copy-start.2
  36.8 0.0 copy-start.3
  36.8 51.5 %all-to-all-done.refs_0_ = bf16[16,144,640]{2,1,0:T(8,128)(2,1)S(1)} async-done(((bf16[16,144,640]{2,1,0:T(8,128)(2,1)}), bf16[16,144,640]{2,1,0:T(8,128)(2,1)S(1)}, u32[]{:S(2)}, u32[]{:S(2)}) %all-to-all-start) | async-done | bytes 2949152 | tf_op jit(solution)/shard_map/all_to_all | solution.py:185
  88.4 0.0 copy-start.1
  88.4 4.8 %all-to-all-start.1 = ((bf16[16,130,640]{2,1,0:T(8,128)(2,1)}), bf16[16,130,640]{2,1,0:T(8,128)(2,1)}, u32[]{:S(2)}, u32[]{:S(2)}) async-start(bf16[16,130,640]{2,1,0:T(8,128)(2,1)} %pack1.1), calls=%async_computation.1 | async-start | bytes 5570560 | tf_op jit(solution)/shard_map/all_to_all | solution.py:185
  93.1 0.0 copy-done.4
  93.1 0.6 broadcast_in_dim.12.counts_ref
  93.7 0.0 copy-done.5
  93.7 0.6 dynamic_slice.6.waves_ref
  94.4 0.0 copy-done.6
  94.4 0.8 copy.19.rates_ref
  95.1 0.0 copy-done.2
  95.2 0.7 copy.16
  95.9 0.0 copy-done.3
  95.9 0.7 copy.17
  96.6 0.0 copy-done.1
  96.6 28.5 %legendre.2 = (bf16[8,137,1280]{2,1,0:T(8,128)(2,1)}, bf16[16,137,640]{2,1,0:T(8,128)(2,1)}) custom-call(s32[8]{0:T(128)} %dynamic_slice.6.waves_ref, s32[1,1280]{1,0:T(1,128)} %broadcast_in_dim.12.counts_ref, f32[137,1]{1,0:T(8,128)} %copy.19.rates_ref, bf16[137,137]{1,0:T(8,128)(2,1)} %bitcast.22, bf16[137,137]{1,0:T(8,128)(2,1)} %bitcast.24, ...), custom_call_target="tpu_custom_call" | custom-call | flops 14365491200 | bytes 26214400 | tf_op jit(solution)/shard_map/legendre/pallas_call | solution.py:130
  125.1 30.3 %all-to-all-done.1.refs_1_ = bf16[16,130,640]{2,1,0:T(8,128)(2,1)} async-done(((bf16[16,130,640]{2,1,0:T(8,128)(2,1)}), bf16[16,130,640]{2,1,0:T(8,128)(2,1)}, u32[]{:S(2)}, u32[]{:S(2)}) %all-to-all-start.1) | async-done | bytes 2662432 | tf_op jit(solution)/shard_map/all_to_all | solution.py:185
  155.4 4.8 %all-to-all-start.3 = ((bf16[16,137,640]{2,1,0:T(8,128)(2,1)}), bf16[16,137,640]{2,1,0:T(8,128)(2,1)S(1)}, u32[]{:S(2)}, u32[]{:S(2)}) async-start(bf16[16,137,640]{2,1,0:T(8,128)(2,1)} %get-tuple-element.9), calls=%async_computation.3 | async-start | bytes 5898240 | tf_op jit(solution)/shard_map/all_to_all | solution.py:194
  160.2 30.2 %legendre.3 = (bf16[8,137,1280]{2,1,0:T(8,128)(2,1)}, bf16[16,137,640]{2,1,0:T(8,128)(2,1)}) custom-call(s32[8]{0:T(128)} %dynamic_slice.6.waves_ref, s32[1,1280]{1,0:T(1,128)} %broadcast_in_dim.12.counts_ref, f32[137,1]{1,0:T(8,128)} %copy.19.rates_ref, bf16[137,137]{1,0:T(8,128)(2,1)} %bitcast.23, bf16[137,137]{1,0:T(8,128)(2,1)} %bitcast.25, ...), custom_call_target="tpu_custom_call" | custom-call | flops 14365491200 | bytes 26214400 | tf_op jit(solution)/shard_map/legendre/pallas_call | solution.py:130
  190.3 35.5 %all-to-all-done.3.in_ref = bf16[16,137,640]{2,1,0:T(8,128)(2,1)S(1)} async-done(((bf16[16,137,640]{2,1,0:T(8,128)(2,1)}), bf16[16,137,640]{2,1,0:T(8,128)(2,1)S(1)}, u32[]{:S(2)}, u32[]{:S(2)}) %all-to-all-start.3) | async-done | bytes 2805792 | tf_op jit(solution)/shard_map/all_to_all | solution.py:194
  225.9 0.0 copy-start
  225.9 4.8 %all-to-all-start.2 = ((bf16[16,137,640]{2,1,0:T(8,128)(2,1)}), bf16[16,137,640]{2,1,0:T(8,128)(2,1)}, u32[]{:S(2)}, u32[]{:S(2)}) async-start(bf16[16,137,640]{2,1,0:T(8,128)(2,1)} %get-tuple-element.8), calls=%async_computation.2 | async-start | bytes 5898240 | tf_op jit(solution)/shard_map/all_to_all | solution.py:194
  230.6 3.5 %maximum_bitcast_fusion = bf16[8,1280,274]{1,2,0:T(8,128)(2,1)S(1)} fusion(bf16[137,8,1280]{2,0,1:T(8,128)(2,1)} %bitcast.21, bf16[137,8,1280]{2,0,1:T(8,128)(2,1)} %bitcast.20), kind=kLoop, calls=%fused_computation | loop fusion | flops 11223040 | bytes 11223040 | tf_op jit(solution)/shard_map/transpose | solution.py:197
  234.2 0.0 copy-done
  234.2 3.6 %copy.22 = bf16[8,1280,274]{1,0,2:T(8,128)(2,1)} copy(bf16[8,1280,274]{1,2,0:T(8,128)(2,1)S(1)} %maximum_bitcast_fusion) | data formatting | bytes 11223040
  237.7 8.9 %unpack0.1.refs_0_ = bf16[2,137,80,128]{3,2,1,0:T(8,128)(2,1)} custom-call(bf16[16,137,640]{2,1,0:T(8,128)(2,1)} %copy-done), custom_call_target="tpu_custom_call" | custom-call | bytes 5611520 | tf_op jit(solution)/shard_map/unpack0/pallas_call | solution.py:70
  246.7 49.8 %all-to-all-done.2.in_ref = bf16[16,137,640]{2,1,0:T(8,128)(2,1)} async-done(((bf16[16,137,640]{2,1,0:T(8,128)(2,1)}), bf16[16,137,640]{2,1,0:T(8,128)(2,1)}, u32[]{:S(2)}, u32[]{:S(2)}) %all-to-all-start.2) | async-done | bytes 2805792 | tf_op jit(solution)/shard_map/all_to_all | solution.py:194
  296.4 8.9 %unpack1.1 = bf16[2,137,80,128]{3,2,1,0:T(8,128)(2,1)} custom-call(bf16[16,137,640]{2,1,0:T(8,128)(2,1)} %all-to-all-done.2.in_ref, bf16[2,137,80,128]{3,2,1,0:T(8,128)(2,1)} %unpack0.1.refs_0_), custom_call_target="tpu_custom_call", output_to_operand_aliasing={{}: (1, {})} | custom-call | bytes 5611520 | tf_op jit(solution)/shard_map/unpack1/pallas_call | solution.py:70
Async XLA Ops:
  16.2 72.2 %all-to-all-start = ((bf16[16,144,640]{2,1,0:T(8,128)(2,1)}), bf16[16,144,640]{2,1,0:T(8,128)(2,1)S(1)}, u32[]{:S(2)}, u32[]{:S(2)}) async-start(bf16[16,144,640]{2,1,0:T(8,128)(2,1)} %pack0.1), calls=%async_computation | async-start | bytes 5898240 | tf_op jit(solution)/shard_map/all_to_all | solution.py:185
  22.7 70.5 %copy-start.4 = (s32[1280]{0:T(1024)S(1)}, s32[1280]{0:T(1024)}, u32[]{:S(2)}) copy-start(s32[1280]{0:T(1024)} %param.10) | copy-start | bytes 15364
  22.7 71.1 %copy-start.5 = (s32[128]{0:T(128)S(1)}, s32[128]{0:T(128)}, u32[]{:S(2)}) copy-start(s32[128]{0:T(128)} %param.11) | copy-start | bytes 1540
  22.7 71.7 %copy-start.6 = (f32[137]{0:T(256)S(1)}, f32[137]{0:T(256)}, u32[]{:S(2)}) copy-start(f32[137]{0:T(256)} %param.13) | copy-start | bytes 1648
  36.8 58.3 %copy-start.2 = (bf16[137,137]{1,0:T(8,128)(2,1)S(1)}, bf16[137,137]{1,0:T(8,128)(2,1)}, u32[]{:S(2)}) copy-start(bf16[137,137]{1,0:T(8,128)(2,1)} %param.14) | copy-start | bytes 112618
  36.8 59.0 %copy-start.3 = (bf16[137,137]{1,0:T(8,128)(2,1)S(1)}, bf16[137,137]{1,0:T(8,128)(2,1)}, u32[]{:S(2)}) copy-start(bf16[137,137]{1,0:T(8,128)(2,1)} %param.15) | copy-start | bytes 112618
  88.4 8.3 %copy-start.1 = (bf16[16,144,640]{2,1,0:T(8,128)(2,1)}, bf16[16,144,640]{2,1,0:T(8,128)(2,1)S(1)}, u32[]{:S(2)}) copy-start(bf16[16,144,640]{2,1,0:T(8,128)(2,1)S(1)} %all-to-all-done.refs_0_) | copy-start | bytes 8847364
  88.4 67.0 %all-to-all-start.1 = ((bf16[16,130,640]{2,1,0:T(8,128)(2,1)}), bf16[16,130,640]{2,1,0:T(8,128)(2,1)}, u32[]{:S(2)}, u32[]{:S(2)}) async-start(bf16[16,130,640]{2,1,0:T(8,128)(2,1)} %pack1.1), calls=%async_computation.1 | async-start | bytes 5570560 | tf_op jit(solution)/shard_map/all_to_all | solution.py:185
  155.4 70.5 %all-to-all-start.3 = ((bf16[16,137,640]{2,1,0:T(8,128)(2,1)}), bf16[16,137,640]{2,1,0:T(8,128)(2,1)S(1)}, u32[]{:S(2)}, u32[]{:S(2)}) async-start(bf16[16,137,640]{2,1,0:T(8,128)(2,1)} %get-tuple-element.9), calls=%async_computation.3 | async-start | bytes 5898240 | tf_op jit(solution)/shard_map/all_to_all | solution.py:194
  225.9 8.3 %copy-start = (bf16[16,137,640]{2,1,0:T(8,128)(2,1)}, bf16[16,137,640]{2,1,0:T(8,128)(2,1)S(1)}, u32[]{:S(2)}) copy-start(bf16[16,137,640]{2,1,0:T(8,128)(2,1)S(1)} %all-to-all-done.3.in_ref) | copy-start | bytes 8417284
  225.9 70.6 %all-to-all-start.2 = ((bf16[16,137,640]{2,1,0:T(8,128)(2,1)}), bf16[16,137,640]{2,1,0:T(8,128)(2,1)}, u32[]{:S(2)}, u32[]{:S(2)}) async-start(bf16[16,137,640]{2,1,0:T(8,128)(2,1)} %get-tuple-element.8), calls=%async_computation.2 | async-start | bytes 5898240 | tf_op jit(solution)/shard_map/all_to_all | solution.py:194
